TPU v7x, 256 devices: a whole 4x4x8 slice. The times are simulated.
256 devices in a mesh: pair: 8 (over z), intg: 32 (over y, x, core).
Axes of the slice: x: 4, y: 4, z: 8, core: 2. Of those that a mesh axis runs over, the one named last changes fastest.
Arguments:
- amplitudes: bfloat16 [3072, 32768], P('pair', 'intg'), may hold values from -6 to 6
- integrals: bfloat16 [8192, 32768], P('pair', 'intg'), may hold values from -0.0625 to 0.0625
- sym_rows: int32 [64], P('pair'), may hold values from 0 to 3
- sym_cols: int32 [256], P('intg'), may hold values from 0 to 3
- mirror_rows: int32 [8192], replicated, may hold values from 0 to 8191, as said below
Outputs:
- residual: bfloat16 [3072, 8192], P('intg', 'pair')
Inputs may be any that keep to these rules, and one draw needn't show every extreme that they name: `mirror_rows`: an involution without fixed points; it maps the rows of each 128-row tile onto all rows of one other tile.
All inputs are finite; a program needn't handle non-finite values.
Results may differ from a plain program's by a relative error of at most 0.001.
Values may be sent and summed in bfloat16 or wider, within the bound.
No kernel may reach another device: no remote copies, remote signals or barrier semaphores. Data moves between devices by JAX's collectives and lax.ppermute only.
A program may use at most 128 MiB of HBM per device.

v0:
```python
import functools

import jax
import jax.numpy as jnp
from jax import lax
from jax.experimental import pallas as pl
from jax.experimental.pallas import tpu as pltpu
from jax.sharding import Mesh, PartitionSpec as P


TILE = 128
SWAP = ((0, 1), (1, 0))


def shift(n, d):
    return [(i, (i + d) % n) for i in range(n)]


def cross(n, d):
    return [(2 * i + c, 2 * ((i + d) % n) + 1 - c) for i in range(n) for c in range(2)]


def pick(array, index, axis):
    return lax.dynamic_index_in_dim(array, index, axis, keepdims=False)


def scatter_ring(part, axis, early):
    far = part(2)
    half = far.shape[0] // 2
    rest = [(0, 0)] * (far.ndim - 1)
    send_up = functools.partial(lax.ppermute, axis_name=axis, perm=shift(4, 1))
    send_down = functools.partial(lax.ppermute, axis_name=axis, perm=shift(4, -1))
    from_up = send_up(far[:half])
    from_down = send_down(far[half:])
    up, down = part(1), part(3)
    if not early:
        up = send_up(up + jnp.pad(from_up, [(0, half), *rest]))
        down = send_down(down + jnp.pad(from_down, [(half, 0), *rest]))
        return part(0) + up + down
    up_now = send_up(up[half:])
    down_now = send_down(down[:half])
    up = send_up(up[:half] + from_up)
    down = send_down(down[half:] + from_down)
    return (
        part(0)
        + jnp.pad(up + down_now, [(0, half), *rest])
        + jnp.pad(down + up_now, [(half, 0), *rest])
    )


def product_kernel(size, count, *refs):
    blocks, given = refs[: 2 * count], refs[2 * count : 2 * count + 2]
    *out_refs, a_ref, v_own, v_other, sems = refs[-6:]
    v_refs = (v_own, v_other)
    rows, k = blocks[0].shape
    half = 2 * size * count
    copies = [pltpu.make_async_copy(src, dst, sems.at[i]) for i, (src, dst) in enumerate(zip(given, v_refs))]
    for i, block in enumerate(blocks):
        level, h = divmod(i, 2)
        for part in range(2):
            for pair in range(2):
                into, of = part * half + (2 * level + pair) * size, pair * rows // 2 + part * size
                copies.append(
                    pltpu.make_async_copy(
                        block.at[of : of + size, :],
                        a_ref.at[into : into + size, h * k : (h + 1) * k],
                        sems.at[len(copies)],
                    )
                )
    for copy in copies:
        copy.start()
    for copy in copies:
        copy.wait()
    wide = 512

    def column(n, carry):
        at = pl.ds(pl.multiple_of(n * wide, wide), wide)
        sums = sum(
            lax.dot_general(
                a_ref[:, h * k : (h + 1) * k], v_ref[at, :], (((1,), (1,)), ((), ())),
                preferred_element_type=jnp.float32,
            )
            for h, v_ref in enumerate(v_refs)
        )
        for part, out_ref in enumerate(out_refs):
            out_ref[:, :, at] = sums[part * half : (part + 1) * half].reshape(count, 2 * size, wide)
        return carry

    lax.fori_loop(0, v_refs[0].shape[0] // wide, column, 0)


def product(blocks, v, group, levels, sums):
    rows, k = blocks[0].shape
    count, size, ab = len(blocks) // 2, rows // 4, v[0].shape[0]
    place = pl.BlockSpec((count, 2 * size, ab), lambda i: (group, 0, 0))
    n = len(blocks) + 2
    return pl.pallas_call(
        functools.partial(product_kernel, size, count),
        grid=(1,),
        out_shape=[jax.ShapeDtypeStruct((levels, 2 * size, ab), jnp.float32)] * 2,
        in_specs=[pl.BlockSpec(memory_space=pl.ANY)] * (n + len(sums)),
        out_specs=[place] * 2,
        scratch_shapes=[
            pltpu.VMEM((count * rows, 2 * k), v[0].dtype),
            *[pltpu.VMEM(t.shape, t.dtype) for t in v],
            pltpu.SemaphoreType.DMA((2 + 4 * len(blocks),)),
        ],
        input_output_aliases={n + i: i for i in range(len(sums))},
        compiler_params=pltpu.CompilerParams(vmem_limit_bytes=28 << 20),
        cost_estimate=pl.CostEstimate(
            flops=4 * count * rows * ab * k,
            bytes_accessed=4 * count * rows * k + 4 * ab * k + 4 * count * rows * ab,
            transcendentals=0,
        ),
    )(*blocks, *v, *sums)


def mirror_kernel(tile_ref, lane_ref, given_ref, out_ref, sum_ref, sem):
    copy = pltpu.make_async_copy(given_ref, sum_ref, sem)
    copy.start()
    copy.wait()
    rows = sum_ref.shape[1]
    for t in range(64):
        twin = tile_ref[t]
        twin_column = pl.multiple_of((twin % 8) * TILE, TILE)
        own = sum_ref[t // 8, :, (t % 8) * TILE : (t % 8 + 1) * TILE]
        other = sum_ref[twin // 8, :, pl.ds(twin_column, TILE)]
        lanes = jnp.broadcast_to(lane_ref[t : t + 1, :], (rows, TILE))
        other = jnp.take_along_axis(other, lanes, axis=1)
        out_ref[t // 8, :, (t % 8) * TILE : (t % 8 + 1) * TILE] = (own - other).astype(out_ref.dtype)


def antisymmetrize(sums, mirror_rows):
    tiles = mirror_rows.reshape(-1, TILE)
    twin = tiles[:, 0] // TILE
    lanes = tiles % TILE
    return pl.pallas_call(
        mirror_kernel,
        out_shape=jax.ShapeDtypeStruct(sums.shape, jnp.bfloat16),
        in_specs=[
            pl.BlockSpec(memory_space=pltpu.SMEM),
            pl.BlockSpec(memory_space=pltpu.VMEM),
            pl.BlockSpec(memory_space=pl.ANY),
        ],
        out_specs=pl.BlockSpec(memory_space=pltpu.VMEM),
        scratch_shapes=[pltpu.VMEM(sums.shape, sums.dtype), pltpu.SemaphoreType.DMA],
        compiler_params=pltpu.CompilerParams(vmem_limit_bytes=8 << 20),
    )(twin, lanes, sums)


def in_layer(levels, *args):
    return shards(levels, *args)


def shards(levels, a, v, sym_rows, sym_cols, mirror_rows):
    z, y, x, c = (lax.axis_index(n) for n in "zyxc")
    ab, k = v.shape
    row_sym = jnp.repeat(sym_rows, TILE)

    def allowed(values, symmetry):
        col_sym = jnp.repeat(symmetry, TILE)
        return jnp.where(row_sym[:, None] == col_sym[None, :], values, jnp.zeros((), values.dtype))

    over = functools.partial(lax.ppermute, axis_name="c", perm=SWAP)
    v_over, sym_over = over(v), over(sym_cols)

    rows = a.shape[0] // 4
    size = rows // 2
    quads = a.reshape(2, 2, rows, k)
    mine, theirs = pick(quads, c, 1), pick(quads, 1 - c, 1)
    swapped = over(theirs)
    both = (allowed(v, sym_cols), allowed(v_over, sym_over))

    middle = levels // 2
    at_home = [t.reshape(2 * rows, k) for t in (mine, theirs)]
    moving = {(h, d): at_home[h] for h in range(2) for d in (1, -1)}
    blocks = [{0: t.reshape(2 * rows, k)} for t in (mine, swapped)]
    near = [r % levels for r in range(-2, 2)]
    far = [r % levels for r in range(2, levels - 2)]
    gathered = lambda group: [blocks[h][r] for r in group for h in range(2)]
    sums = ()
    for s in range(1, middle + 1):
        for h in range(2):
            ways = (1, -1) if s < middle else (1 - 2 * h,)
            if h and s == 3:
                sums = product(gathered(near), both, 0, levels, sums)
            for d in ways:
                if h and s == 1:
                    got = lax.ppermute(moving[h, d], ("z", "c"), cross(levels, d))
                else:
                    got = lax.ppermute(moving[h, d], "z", shift(levels, d))
                moving[h, d] = blocks[h][-s * d % levels] = got
    sums = product(gathered(far), both, 1, levels, sums)

    first = sums[0].reshape(4, 2, 2, size, ab)

    def parity(at):
        return (at // 2 - z) % 2

    def of_x(o):
        at = (x + o) % 4
        piece = lax.dynamic_slice(first, (0, parity(at), at % 2, 0, 0), (4, 1, 1, size, ab))
        return piece.reshape(4, size, ab)

    summed = scatter_ring(of_x, "x", True)
    turn = (x // 2 - z - parity(x)) // 2 + 1
    first = scatter_ring(lambda o: pick(summed, (y + o + turn) % 4, 0), "y", False)

    second = sums[1].reshape(levels, 2, size, ab)

    def of_y(o):
        at = 2 * (y + o) - z + 2
        return jnp.concatenate([pick(second, (at + i) % levels, 0) for i in range(2)])

    summed_y = scatter_ring(of_y, "y", True)
    second = scatter_ring(lambda o: pick(summed_y, (x + o) % 4, 0), "x", False)
    sums = jnp.concatenate([first, second], axis=0)

    share = rows // levels
    spread = lax.all_to_all(sums.reshape(levels, share, ab), "z", 0, 0)
    result = antisymmetrize(spread, mirror_rows)
    return lax.all_to_all(result, "z", 0, 0).reshape(rows, ab)


def solution(mesh):
    levels = mesh.shape["pair"]
    grid = Mesh(mesh.devices.reshape(levels, 4, 4, 2), ("z", "y", "x", "c"))
    plane = ("y", "x", "c")
    return jax.shard_map(
        functools.partial(in_layer, levels),
        mesh=grid,
        in_specs=(P("z", plane), P("z", plane), P("z"), P(plane), P()),
        out_specs=P(plane, "z"),
        check_vma=False,
    )
```

profile of v0, /device:TPU:6, one launch (start us, length us, event | category | flops | bytes accessed | tf_op | source)
XLA Modules:
  0.0 169.3 jit_solution(3135205448416474126)
XLA Ops:
  1.2 6.0 %collective-permute-start.2 = (bf16[192,1024]{1,0:T(8,128)(2,1)S(1)}, bf16[192,1024]{1,0:T(8,128)(2,1)S(1)}, u32[]{:S(2)}, u32[]{:S(2)}) collective-permute-start(bf16[192,1024]{1,0:T(8,128)(2,1)S(1)} %bitcast.105), channel_id=1, source_target_pairs={{0,225},{1,224},{32,1},{33,0},{64,33},{65,32},{96,65},{97,64},{128... | collective-permute-start | bytes 1179656 | tf_op jit(solution)/shard_map/ppermute | solution.py:189
  8.5 3.2 %collective-permute-start = (bf16[192,1024]{1,0:T(8,128)(2,1)S(1)}, bf16[192,1024]{1,0:T(8,128)(2,1)S(1)}, u32[]{:S(2)}, u32[]{:S(2)}) collective-permute-start(bf16[192,1024]{1,0:T(8,128)(2,1)S(1)} %bitcast.101), channel_id=1, source_target_pairs={{0,224},{32,0},{64,32},{96,64},{128,96},{160,128},{192,160},{224,1... | collective-permute-start | bytes 1179656 | tf_op jit(solution)/shard_map/ppermute | solution.py:191
  11.8 5.0 %collective-permute-done.2.refs_7_ = bf16[192,1024]{1,0:T(8,128)(2,1)S(1)} collective-permute-done((bf16[192,1024]{1,0:T(8,128)(2,1)S(1)}, bf16[192,1024]{1,0:T(8,128)(2,1)S(1)}, u32[]{:S(2)}, u32[]{:S(2)}) %collective-permute-start.2) | collective-permute-done | bytes 393248 | tf_op jit(solution)/shard_map/ppermute | solution.py:189
  20.4 6.5 %collective-permute-done.11.refs_3_ = bf16[192,1024]{1,0:T(8,128)(2,1)S(1)} collective-permute-done((bf16[192,1024]{1,0:T(8,128)(2,1)S(1)}, bf16[192,1024]{1,0:T(8,128)(2,1)S(1)}, u32[]{:S(2)}, u32[]{:S(2)}) %collective-permute-start.11) | collective-permute-done | bytes 393248 | tf_op jit(solution)/shard_map/ppermute | solution.py:189
  26.9 3.2 %collective-permute-start.1 = (bf16[192,1024]{1,0:T(8,128)(2,1)S(1)}, bf16[192,1024]{1,0:T(8,128)(2,1)S(1)}, u32[]{:S(2)}, u32[]{:S(2)}) collective-permute-start(bf16[192,1024]{1,0:T(8,128)(2,1)S(1)} %collective-permute-done.refs_6_), channel_id=1, source_target_pairs={{0,224},{32,0},{64,32},{96,64},{128,96},{160,128},{192,160},{224,1... | collective-permute-start | bytes 1179656 | tf_op jit(solution)/shard_map/ppermute | solution.py:191
  30.2 3.4 %collective-permute-done.3.refs_1_ = bf16[192,1024]{1,0:T(8,128)(2,1)S(1)} collective-permute-done((bf16[192,1024]{1,0:T(8,128)(2,1)S(1)}, bf16[192,1024]{1,0:T(8,128)(2,1)S(1)}, u32[]{:S(2)}, u32[]{:S(2)}) %collective-permute-start.3) | collective-permute-done | bytes 393248 | tf_op jit(solution)/shard_map/ppermute | solution.py:191
  33.6 3.7 %collective-permute-start.5 = (bf16[192,1024]{1,0:T(8,128)(2,1)S(1)}, bf16[192,1024]{1,0:T(8,128)(2,1)S(1)}, u32[]{:S(2)}, u32[]{:S(2)}) collective-permute-start(bf16[192,1024]{1,0:T(8,128)(2,1)S(1)} %collective-permute-done.3.refs_1_), channel_id=1, source_target_pairs={{0,224},{32,0},{64,32},{96,64},{128,96},{160,128},{192,160},{224,1... | collective-permute-start | bytes 1179656 | tf_op jit(solution)/shard_map/ppermute | solution.py:191
  38.2 7.5 %collective-permute-done.12.refs_1_ = bf16[192,1024]{1,0:T(8,128)(2,1)S(1)} collective-permute-done((bf16[192,1024]{1,0:T(8,128)(2,1)S(1)}, bf16[192,1024]{1,0:T(8,128)(2,1)S(1)}, u32[]{:S(2)}, u32[]{:S(2)}) %collective-permute-start.12) | collective-permute-done | bytes 393248 | tf_op jit(solution)/shard_map/ppermute | solution.py:191
  45.7 4.0 %collective-permute-done.5.refs_3_ = bf16[192,1024]{1,0:T(8,128)(2,1)S(1)} collective-permute-done((bf16[192,1024]{1,0:T(8,128)(2,1)S(1)}, bf16[192,1024]{1,0:T(8,128)(2,1)S(1)}, u32[]{:S(2)}, u32[]{:S(2)}) %collective-permute-start.5) | collective-permute-done | bytes 393248 | tf_op jit(solution)/shard_map/ppermute | solution.py:191
  49.8 3.7 %collective-permute-start.4 = (bf16[192,1024]{1,0:T(8,128)(2,1)S(1)}, bf16[192,1024]{1,0:T(8,128)(2,1)S(1)}, u32[]{:S(2)}, u32[]{:S(2)}) collective-permute-start(bf16[192,1024]{1,0:T(8,128)(2,1)S(1)} %collective-permute-done.1.refs_0_), channel_id=1, source_target_pairs={{0,224},{32,0},{64,32},{96,64},{128,96},{160,128},{192,160},{224,1... | collective-permute-start | bytes 1179656 | tf_op jit(solution)/shard_map/ppermute | solution.py:191
  56.2 2.9 %compare_select_fusion = (bf16[1024,1024]{1,0:T(8,128)(2,1)S(1)}, bf16[1024,1024]{1,0:T(8,128)(2,1)S(1)}) fusion(bf16[1024,1024]{1,0:T(8,128)(2,1)} %collective-permute-done.15, s32[1024]{0:T(1024)S(1)} %broadcast_bitcast_fusion, s32[1024]{0:T(1024)S(1)} %get-tuple-element.40, bf16[1024,1024]{1,0:T(8,128)(2,1)} %param.6, s32[1024]{0:T(1024)S(1)} %get-tuple-element.39), kind=kLoop, calls=%fused_computation | loop fusion | flops 4194304 | bytes 8400896 | tf_op jit(solution)/shard_map/jit(_where)/select_n | solution.py:162
  64.1 5.0 %shard_map.55 = (f32[8,96,1024]{2,1,0:T(8,128)S(1)}, f32[8,96,1024]{2,1,0:T(8,128)S(1)}) custom-call(bf16[192,1024]{1,0:T(8,128)(2,1)S(1)} %copy-done.12, bf16[192,1024]{1,0:T(8,128)(2,1)S(1)} %collective-permute-done.12.refs_1_, bf16[192,1024]{1,0:T(8,128)(2,1)S(1)} %copy-done.6, bf16[192,1024]{1,0:T(8,128)(2,1)S(1)} %copy-done.8, ...), custom_call_target="tpu_custom_call" | custom-call | flops 3221225472 | bytes 10485760 | tf_op jit(solution)/shard_map/pallas_call | solution.py:97
  70.0 5.0 %shard_map.56 = (f32[8,96,1024]{2,1,0:T(8,128)S(1)}, f32[8,96,1024]{2,1,0:T(8,128)S(1)}) custom-call(bf16[192,1024]{1,0:T(8,128)(2,1)S(1)} %collective-permute-done.1.refs_0_, bf16[192,1024]{1,0:T(8,128)(2,1)S(1)} %copy-done.2, bf16[192,1024]{1,0:T(8,128)(2,1)S(1)} %collective-permute-done.4.refs_2_, ...), custom_call_target="tpu_custom_call", output_to_operand_aliasing={{0}: (10, {}), {1}: (11, {})} | custom-call | flops 3221225472 | bytes 10485760 | tf_op jit(solution)/shard_map/pallas_call | solution.py:97
  79.9 2.9 %dynamic-slice_bitcast_fusion.8 = (f32[2,48,1024]{2,1,0:T(8,128)}, f32[2,48,1024]{2,1,0:T(8,128)}, f32[2,48,1024]{2,1,0:T(8,128)}, f32[2,48,1024]{2,1,0:T(8,128)...) fusion(f32[8,2,48,1024]{3,2,1,0:T(8,128)} %bitcast.98, s32[]{:T(128)S(6)} %select_n.280, s32[]{:T(128)S(6)} %select_n.286, ...), kind=kLoop, calls=%fused_computation.19 | loop fusion | bytes 4718616 | tf_op jit(solution)/shard_map/jit(dynamic_index_in_dim)/squeeze | solution.py:24
  93.9 3.3 %collective-permute-start.29 = (f32[2,48,1024]{2,1,0:T(8,128)}, f32[2,48,1024]{2,1,0:T(8,128)}, u32[]{:S(2)}, u32[]{:S(2)}) collective-permute-start(f32[2,48,1024]{2,1,0:T(8,128)} %get-tuple-element.19), channel_id=1, source_target_pairs={{0,24},{8,0},{16,8},{24,16},{1,25},{9,1},{17,9},{25,17},{2,26},{10... | collective-permute-start | bytes 1179656 | tf_op jit(solution)/shard_map/ppermute | solution.py:41
  103.4 3.0 %collective-permute-done.18 = f32[2,48,1024]{2,1,0:T(8,128)} collective-permute-done((f32[2,48,1024]{2,1,0:T(8,128)}, f32[2,48,1024]{2,1,0:T(8,128)}, u32[]{:S(2)}, u32[]{:S(2)}) %collective-permute-start.18) | collective-permute-done | bytes 393248 | tf_op jit(solution)/shard_map/ppermute | solution.py:42
  106.3 3.0 %collective-permute-start.31 = (f32[2,48,1024]{2,1,0:T(8,128)}, f32[2,48,1024]{2,1,0:T(8,128)}, u32[]{:S(2)}, u32[]{:S(2)}) collective-permute-start(f32[2,48,1024]{2,1,0:T(8,128)} %get-tuple-element.26), channel_id=1, source_target_pairs={{0,24},{8,0},{16,8},{24,16},{1,25},{9,1},{17,9},{25,17},{2,26},{10... | collective-permute-start | bytes 1179656 | tf_op jit(solution)/shard_map/ppermute | solution.py:43
  112.0 3.2 %collective-permute-start.25 = (f32[24,1024]{1,0:T(8,128)S(1)}, f32[24,1024]{1,0:T(8,128)S(1)}, u32[]{:S(2)}, u32[]{:S(2)}) collective-permute-start(f32[24,1024]{1,0:T(8,128)S(1)} %get-tuple-element.30), channel_id=1, source_target_pairs={{0,24},{8,0},{16,8},{24,16},{1,25},{9,1},{17,9},{25,17},{2,26},{10... | collective-permute-start | bytes 294920 | tf_op jit(solution)/shard_map/ppermute | solution.py:34
  115.2 3.5 %collective-permute-done.28 = f32[2,48,1024]{2,1,0:T(8,128)} collective-permute-done((f32[2,48,1024]{2,1,0:T(8,128)}, f32[2,48,1024]{2,1,0:T(8,128)}, u32[]{:S(2)}, u32[]{:S(2)}) %collective-permute-start.28) | collective-permute-done | bytes 393248 | tf_op jit(solution)/shard_map/ppermute | solution.py:42
  123.5 3.2 %collective-permute-start.26 = (f32[48,1024]{1,0:T(8,128)S(1)}, f32[48,1024]{1,0:T(8,128)S(1)}, u32[]{:S(2)}, u32[]{:S(2)}) collective-permute-start(f32[48,1024]{1,0:T(8,128)S(1)} %get-tuple-element.28), channel_id=1, source_target_pairs={{0,24},{8,0},{16,8},{24,16},{1,25},{9,1},{17,9},{25,17},{2,26},{10... | collective-permute-start | bytes 589832 | tf_op jit(solution)/shard_map/ppermute | solution.py:38
  132.8 2.7 %collective-permute-done.34 = f32[48,1024]{1,0:T(8,128)S(1)} collective-permute-done((f32[48,1024]{1,0:T(8,128)S(1)}, f32[48,1024]{1,0:T(8,128)S(1)}, u32[]{:S(2)}, u32[]{:S(2)}) %collective-permute-start.34) | collective-permute-done | bytes 196640 | tf_op jit(solution)/shard_map/ppermute | solution.py:37
  137.8 3.5 %all-to-all-start = ((f32[8,12,1024]{2,1,0:T(8,128)}), f32[8,12,1024]{2,1,0:T(8,128)S(1)}, u32[]{:S(2)}, u32[]{:S(2)}) async-start(f32[8,12,1024]{2,1,0:T(8,128)} %reshape.57), calls=%async_computation | async-start | bytes 1048576 | tf_op jit(solution)/shard_map/all_to_all | solution.py:220
  141.5 13.1 %all-to-all-done.given_ref = f32[8,12,1024]{2,1,0:T(8,128)S(1)} async-done(((f32[8,12,1024]{2,1,0:T(8,128)}), f32[8,12,1024]{2,1,0:T(8,128)S(1)}, u32[]{:S(2)}, u32[]{:S(2)}) %all-to-all-start) | async-done | bytes 393248 | tf_op jit(solution)/shard_map/all_to_all | solution.py:220
  155.7 12.9 %all_to_all.10 = bf16[8,12,1024]{2,1,0:T(8,128)(2,1)S(1)} all-to-all(bf16[8,12,1024]{2,1,0:T(8,128)(2,1)S(1)} %shard_map.57), channel_id=1, replica_groups=mesh['z'=8,'y'=4,'x'=4,'c'=2] {'z'}, dimensions={0} | all-to-all | bytes 393216 | tf_op jit(solution)/shard_map/all_to_all | solution.py:222
  (114 shorter events, 55.6 us)
Async XLA Ops:
  0.0 54.1 %collective-permute-start.15 = (bf16[1024,1024]{1,0:T(8,128)(2,1)}, bf16[1024,1024]{1,0:T(8,128)(2,1)}, u32[]{:S(2)}, u32[]{:S(2)}) collective-permute-start(bf16[1024,1024]{1,0:T(8,128)(2,1)} %param.6), channel_id=1, source_target_pairs={{0,1},{1,0},{2,3},{3,2},{4,5},{5,4},{6,7},{7,6},{8,9},{9,8},{10,11... | collective-permute-start | bytes 6291464 | tf_op jit(solution)/shard_map/ppermute | solution.py:165
  1.2 15.6 %collective-permute-start.2 = (bf16[192,1024]{1,0:T(8,128)(2,1)S(1)}, bf16[192,1024]{1,0:T(8,128)(2,1)S(1)}, u32[]{:S(2)}, u32[]{:S(2)}) collective-permute-start(bf16[192,1024]{1,0:T(8,128)(2,1)S(1)} %bitcast.105), channel_id=1, source_target_pairs={{0,225},{1,224},{32,1},{33,0},{64,33},{65,32},{96,65},{97,64},{128... | collective-permute-start | bytes 1179656 | tf_op jit(solution)/shard_map/ppermute | solution.py:189
  7.2 13.2 %collective-permute-start.6 = (bf16[192,1024]{1,0:T(8,128)(2,1)S(1)}, bf16[192,1024]{1,0:T(8,128)(2,1)S(1)}, u32[]{:S(2)}, u32[]{:S(2)}) collective-permute-start(bf16[192,1024]{1,0:T(8,128)(2,1)S(1)} %bitcast.100), channel_id=1, source_target_pairs={{0,32},{32,64},{64,96},{96,128},{128,160},{160,192},{192,224},{224... | collective-permute-start | bytes 1179656 | tf_op jit(solution)/shard_map/ppermute | solution.py:191
  7.2 19.7 %collective-permute-start.11 = (bf16[192,1024]{1,0:T(8,128)(2,1)S(1)}, bf16[192,1024]{1,0:T(8,128)(2,1)S(1)}, u32[]{:S(2)}, u32[]{:S(2)}) collective-permute-start(bf16[192,1024]{1,0:T(8,128)(2,1)S(1)} %bitcast.106), channel_id=1, source_target_pairs={{0,33},{1,32},{32,65},{33,64},{64,97},{65,96},{96,129},{97,128},{1... | collective-permute-start | bytes 1179656 | tf_op jit(solution)/shard_map/ppermute | solution.py:189
  8.5 18.4 %collective-permute-start = (bf16[192,1024]{1,0:T(8,128)(2,1)S(1)}, bf16[192,1024]{1,0:T(8,128)(2,1)S(1)}, u32[]{:S(2)}, u32[]{:S(2)}) collective-permute-start(bf16[192,1024]{1,0:T(8,128)(2,1)S(1)} %bitcast.101), channel_id=1, source_target_pairs={{0,224},{32,0},{64,32},{96,64},{128,96},{160,128},{192,160},{224,1... | collective-permute-start | bytes 1179656 | tf_op jit(solution)/shard_map/ppermute | solution.py:191
  16.7 16.9 %collective-permute-start.3 = (bf16[192,1024]{1,0:T(8,128)(2,1)S(1)}, bf16[192,1024]{1,0:T(8,128)(2,1)S(1)}, u32[]{:S(2)}, u32[]{:S(2)}) collective-permute-start(bf16[192,1024]{1,0:T(8,128)(2,1)S(1)} %collective-permute-done.2.refs_7_), channel_id=1, source_target_pairs={{0,224},{32,0},{64,32},{96,64},{128,96},{160,128},{192,160},{224,1... | collective-permute-start | bytes 1179656 | tf_op jit(solution)/shard_map/ppermute | solution.py:191
  20.4 16.9 %collective-permute-start.7 = (bf16[192,1024]{1,0:T(8,128)(2,1)S(1)}, bf16[192,1024]{1,0:T(8,128)(2,1)S(1)}, u32[]{:S(2)}, u32[]{:S(2)}) collective-permute-start(bf16[192,1024]{1,0:T(8,128)(2,1)S(1)} %collective-permute-done.6.refs_2_), channel_id=1, source_target_pairs={{0,32},{32,64},{64,96},{96,128},{128,160},{160,192},{192,224},{224... | collective-permute-start | bytes 1179656 | tf_op jit(solution)/shard_map/ppermute | solution.py:191
  26.9 18.8 %collective-permute-start.12 = (bf16[192,1024]{1,0:T(8,128)(2,1)S(1)}, bf16[192,1024]{1,0:T(8,128)(2,1)S(1)}, u32[]{:S(2)}, u32[]{:S(2)}) collective-permute-start(bf16[192,1024]{1,0:T(8,128)(2,1)S(1)} %collective-permute-done.11.refs_3_), channel_id=1, source_target_pairs={{0,32},{32,64},{64,96},{96,128},{128,160},{160,192},{192,224},{224... | collective-permute-start | bytes 1179656 | tf_op jit(solution)/shard_map/ppermute | solution.py:191
  26.9 18.8 %collective-permute-start.1 = (bf16[192,1024]{1,0:T(8,128)(2,1)S(1)}, bf16[192,1024]{1,0:T(8,128)(2,1)S(1)}, u32[]{:S(2)}, u32[]{:S(2)}) collective-permute-start(bf16[192,1024]{1,0:T(8,128)(2,1)S(1)} %collective-permute-done.refs_6_), channel_id=1, source_target_pairs={{0,224},{32,0},{64,32},{96,64},{128,96},{160,128},{192,160},{224,1... | collective-permute-start | bytes 1179656 | tf_op jit(solution)/shard_map/ppermute | solution.py:191
  33.6 16.2 %collective-permute-start.5 = (bf16[192,1024]{1,0:T(8,128)(2,1)S(1)}, bf16[192,1024]{1,0:T(8,128)(2,1)S(1)}, u32[]{:S(2)}, u32[]{:S(2)}) collective-permute-start(bf16[192,1024]{1,0:T(8,128)(2,1)S(1)} %collective-permute-done.3.refs_1_), channel_id=1, source_target_pairs={{0,224},{32,0},{64,32},{96,64},{128,96},{160,128},{192,160},{224,1... | collective-permute-start | bytes 1179656 | tf_op jit(solution)/shard_map/ppermute | solution.py:191
  37.3 16.8 %collective-permute-start.8 = (bf16[192,1024]{1,0:T(8,128)(2,1)S(1)}, bf16[192,1024]{1,0:T(8,128)(2,1)S(1)}, u32[]{:S(2)}, u32[]{:S(2)}) collective-permute-start(bf16[192,1024]{1,0:T(8,128)(2,1)S(1)} %collective-permute-done.7.refs_0_), channel_id=1, source_target_pairs={{0,32},{32,64},{64,96},{96,128},{128,160},{160,192},{192,224},{224... | collective-permute-start | bytes 1179656 | tf_op jit(solution)/shard_map/ppermute | solution.py:191
  45.7 13.4 %collective-permute-start.16 = (bf16[2,96,1024]{2,1,0:T(8,128)(2,1)S(1)}, bf16[2,96,1024]{2,1,0:T(8,128)(2,1)S(1)}, u32[]{:S(2)}, u32[]{:S(2)}) collective-permute-start(bf16[2,96,1024]{2,1,0:T(8,128)(2,1)S(1)} %bitcast.107), channel_id=1, source_target_pairs={{0,1},{1,0},{2,3},{3,2},{4,5},{5,4},{6,7},{7,6},{8,9},{9,8},{10,11... | collective-permute-start | bytes 1179656 | tf_op jit(solution)/shard_map/ppermute | solution.py:171
  45.7 23.4 %collective-permute-start.13 = (bf16[192,1024]{1,0:T(8,128)(2,1)S(1)}, bf16[192,1024]{1,0:T(8,128)(2,1)S(1)}, u32[]{:S(2)}, u32[]{:S(2)}) collective-permute-start(bf16[192,1024]{1,0:T(8,128)(2,1)S(1)} %collective-permute-done.12.refs_1_), channel_id=1, source_target_pairs={{0,32},{32,64},{64,96},{96,128},{128,160},{160,192},{192,224},{224... | collective-permute-start | bytes 1179656 | tf_op jit(solution)/shard_map/ppermute | solution.py:191
  49.8 19.3 %collective-permute-start.4 = (bf16[192,1024]{1,0:T(8,128)(2,1)S(1)}, bf16[192,1024]{1,0:T(8,128)(2,1)S(1)}, u32[]{:S(2)}, u32[]{:S(2)}) collective-permute-start(bf16[192,1024]{1,0:T(8,128)(2,1)S(1)} %collective-permute-done.1.refs_0_), channel_id=1, source_target_pairs={{0,224},{32,0},{64,32},{96,64},{128,96},{160,128},{192,160},{224,1... | collective-permute-start | bytes 1179656 | tf_op jit(solution)/shard_map/ppermute | solution.py:191
  54.1 15.7 %collective-permute-start.10 = (bf16[192,1024]{1,0:T(8,128)(2,1)S(1)}, bf16[192,1024]{1,0:T(8,128)(2,1)S(1)}, u32[]{:S(2)}, u32[]{:S(2)}) collective-permute-start(bf16[192,1024]{1,0:T(8,128)(2,1)S(1)} %collective-permute-done.5.refs_3_), channel_id=1, source_target_pairs={{0,224},{32,0},{64,32},{96,64},{128,96},{160,128},{192,160},{224,1... | collective-permute-start | bytes 1179656 | tf_op jit(solution)/shard_map/ppermute | solution.py:191
  54.1 15.9 %collective-permute-start.9 = (bf16[192,1024]{1,0:T(8,128)(2,1)S(1)}, bf16[192,1024]{1,0:T(8,128)(2,1)S(1)}, u32[]{:S(2)}, u32[]{:S(2)}) collective-permute-start(bf16[192,1024]{1,0:T(8,128)(2,1)S(1)} %collective-permute-done.8.refs_6_), channel_id=1, source_target_pairs={{0,32},{32,64},{64,96},{96,128},{128,160},{160,192},{192,224},{224... | collective-permute-start | bytes 1179656 | tf_op jit(solution)/shard_map/ppermute | solution.py:191
  86.0 15.4 %collective-permute-start.19 = (f32[2,48,1024]{2,1,0:T(8,128)}, f32[2,48,1024]{2,1,0:T(8,128)}, u32[]{:S(2)}, u32[]{:S(2)}) collective-permute-start(f32[2,48,1024]{2,1,0:T(8,128)} %get-tuple-element.13), channel_id=1, source_target_pairs={{0,6},{2,0},{4,2},{6,4},{1,7},{3,1},{5,3},{7,5},{8,14},{10,8},{12,... | collective-permute-start | bytes 1179656 | tf_op jit(solution)/shard_map/ppermute | solution.py:41
  88.3 13.5 %collective-permute-start.22 = (f32[2,48,1024]{2,1,0:T(8,128)}, f32[2,48,1024]{2,1,0:T(8,128)}, u32[]{:S(2)}, u32[]{:S(2)}) collective-permute-start(f32[2,48,1024]{2,1,0:T(8,128)} %get-tuple-element.16), channel_id=1, source_target_pairs={{0,2},{2,4},{4,6},{6,0},{1,3},{3,5},{5,7},{7,1},{8,10},{10,12},{12... | collective-permute-start | bytes 1179656 | tf_op jit(solution)/shard_map/ppermute | solution.py:40
  93.9 18.1 %collective-permute-start.29 = (f32[2,48,1024]{2,1,0:T(8,128)}, f32[2,48,1024]{2,1,0:T(8,128)}, u32[]{:S(2)}, u32[]{:S(2)}) collective-permute-start(f32[2,48,1024]{2,1,0:T(8,128)} %get-tuple-element.19), channel_id=1, source_target_pairs={{0,24},{8,0},{16,8},{24,16},{1,25},{9,1},{17,9},{25,17},{2,26},{10... | collective-permute-start | bytes 1179656 | tf_op jit(solution)/shard_map/ppermute | solution.py:41
  97.2 13.3 %collective-permute-start.21 = (f32[2,48,1024]{2,1,0:T(8,128)}, f32[2,48,1024]{2,1,0:T(8,128)}, u32[]{:S(2)}, u32[]{:S(2)}) collective-permute-start(f32[2,48,1024]{2,1,0:T(8,128)} %get-tuple-element.18), channel_id=1, source_target_pairs={{0,6},{2,0},{4,2},{6,4},{1,7},{3,1},{5,3},{7,5},{8,14},{10,8},{12,... | collective-permute-start | bytes 1179656 | tf_op jit(solution)/shard_map/ppermute | solution.py:43
  101.4 18.6 %collective-permute-start.32 = (f32[2,48,1024]{2,1,0:T(8,128)}, f32[2,48,1024]{2,1,0:T(8,128)}, u32[]{:S(2)}, u32[]{:S(2)}) collective-permute-start(f32[2,48,1024]{2,1,0:T(8,128)} %get-tuple-element.20), channel_id=1, source_target_pairs={{0,8},{8,16},{16,24},{24,0},{1,9},{9,17},{17,25},{25,1},{2,10},{10... | collective-permute-start | bytes 1179656 | tf_op jit(solution)/shard_map/ppermute | solution.py:40
  101.8 16.9 %collective-permute-start.28 = (f32[2,48,1024]{2,1,0:T(8,128)}, f32[2,48,1024]{2,1,0:T(8,128)}, u32[]{:S(2)}, u32[]{:S(2)}) collective-permute-start(f32[2,48,1024]{2,1,0:T(8,128)} %get-tuple-element.25), channel_id=1, source_target_pairs={{0,8},{8,16},{16,24},{24,0},{1,9},{9,17},{17,25},{25,1},{2,10},{10... | collective-permute-start | bytes 1179656 | tf_op jit(solution)/shard_map/ppermute | solution.py:42
  106.3 13.6 %collective-permute-start.31 = (f32[2,48,1024]{2,1,0:T(8,128)}, f32[2,48,1024]{2,1,0:T(8,128)}, u32[]{:S(2)}, u32[]{:S(2)}) collective-permute-start(f32[2,48,1024]{2,1,0:T(8,128)} %get-tuple-element.26), channel_id=1, source_target_pairs={{0,24},{8,0},{16,8},{24,16},{1,25},{9,1},{17,9},{25,17},{2,26},{10... | collective-permute-start | bytes 1179656 | tf_op jit(solution)/shard_map/ppermute | solution.py:43
  137.8 16.7 %all-to-all-start = ((f32[8,12,1024]{2,1,0:T(8,128)}), f32[8,12,1024]{2,1,0:T(8,128)S(1)}, u32[]{:S(2)}, u32[]{:S(2)}) async-start(f32[8,12,1024]{2,1,0:T(8,128)} %reshape.57), calls=%async_computation | async-start | bytes 1048576 | tf_op jit(solution)/shard_map/all_to_all | solution.py:220
  (30 other events, 371.7 us)
where the time goes:
time: 170 us; the launch traced here: 169 us
  waiting for transfers between devices  60.6 us (36%)
  starting transfers between devices  56.5 us (33%)
  local copies, waits for them, and re-layouts  14.5 us (9%)
  other arithmetic  13.4 us (8%)
  blocking collectives  12.9 us (8%)
  Pallas kernels  11 us (6%)
    ppermute x12, starting transfers between devices, shards(): got = lax.ppermute(moving[h, d], 'z', shift(levels, d))  18.2 us
    ppermute x12, waiting for transfers between devices, shards(): got = lax.ppermute(moving[h, d], 'z', shift(levels, d))  18 us
    all_to_all x1, waiting for transfers between devices, shards(): spread = lax.all_to_all(sums.reshape(levels, share, ab), 'z', 0, 0)  13.1 us
    all_to_all x1, blocking collectives, shards(): return lax.all_to_all(result, 'z', 0, 0).reshape(rows, ab)  12.9 us
    ppermute x2, waiting for transfers between devices, shards(): got = lax.ppermute(moving[h, d], ('z', 'c'), cross(levels, d))  11.5 us
    pallas_call x2, Pallas kernels, product(): pl.pallas_call(functools.partial(product_kernel, size, count), grid=(1,),...  9.92 us
    ppermute x4, starting transfers between devices, scatter_ring(): from_down = send_down(far[half:])  6.72 us
    unnamed x32, local copies, waits for them, and re-layouts  6.62 us
  transfers between devices with their start and end apart: 38, of which 20 were waited for; matrix products, arithmetic and copies ran while one was open for 11% of the time, Pallas kernels for 3%

commit v1 on v0

--- a/solution.py
+++ b/solution.py
@@ -97,7 +97,10 @@
     return pl.pallas_call(
         functools.partial(product_kernel, size, count),
         grid=(1,),
-        out_shape=[jax.ShapeDtypeStruct((levels, 2 * size, ab), jnp.float32)] * 2,
+        out_shape=[
+            jax.ShapeDtypeStruct((levels, 2 * size, ab), jnp.float32),
+            pltpu.HBM((levels, 2 * size, ab), jnp.float32),
+        ],
         in_specs=[pl.BlockSpec(memory_space=pl.ANY)] * (n + len(sums)),
         out_specs=[place] * 2,
         scratch_shapes=[

time: 170 us -> 170 us (level)
  Pallas kernels: 11 us -> 13.4 us
  waiting for transfers between devices: 60.6 us -> 58.7 us
    pallas_call x2, Pallas kernels: 9.92 us -> 12.3 us  [product(): pl.pallas_call(functools.partial(product_kernel, size, count), grid=(1,),...]
    unnamed x32 -> x30, local copies, waits for them, and re-layouts: 6.62 us -> 5.01 us
  transfers between devices with their start and end apart: 38 -> 38, of which waited for: 20 -> 18; matrix products, arithmetic and copies ran while one was open for 11% -> 11% of each run, Pallas kernels for 3% -> 4%
where the time goes in v1:
time: 170 us; the launch traced here: 169 us
  waiting for transfers between devices  58.7 us (35%)
  starting transfers between devices  57.3 us (34%)
  other arithmetic  13.4 us (8%)
  Pallas kernels  13.4 us (8%)
  local copies, waits for them, and re-layouts  12.9 us (8%)
  blocking collectives  12.9 us (8%)
    ppermute x12, starting transfers between devices, shards(): got = lax.ppermute(moving[h, d], 'z', shift(levels, d))  18.2 us
    ppermute x12, waiting for transfers between devices, shards(): got = lax.ppermute(moving[h, d], 'z', shift(levels, d))  17.1 us
    all_to_all x1, waiting for transfers between devices, shards(): spread = lax.all_to_all(sums.reshape(levels, share, ab), 'z', 0, 0)  13.3 us
    all_to_all x1, blocking collectives, shards(): return lax.all_to_all(result, 'z', 0, 0).reshape(rows, ab)  12.9 us
    pallas_call x2, Pallas kernels, product(): pl.pallas_call(functools.partial(product_kernel, size, count), grid=(1,),...  12.3 us
    ppermute x2, waiting for transfers between devices, shards(): got = lax.ppermute(moving[h, d], ('z', 'c'), cross(levels, d))  11.5 us
    ppermute x4, starting transfers between devices, scatter_ring(): from_down = send_down(far[half:])  6.89 us
    ppermute x2, waiting for transfers between devices, scatter_ring(): up = send_up(up[:half] + from_up)  6.06 us
  transfers between devices with their start and end apart: 38, of which 18 were waited for; matrix products, arithmetic and copies ran while one was open for 11% of the time, Pallas kernels for 4%

profile of v1, /device:TPU:6, one launch (start us, length us, event | category | flops | bytes accessed | tf_op | source)
XLA Modules:
  0.0 168.9 jit_solution(10964343078184434071)
XLA Ops:
  1.2 6.0 %collective-permute-start.2 = (bf16[192,1024]{1,0:T(8,128)(2,1)S(1)}, bf16[192,1024]{1,0:T(8,128)(2,1)S(1)}, u32[]{:S(2)}, u32[]{:S(2)}) collective-permute-start(bf16[192,1024]{1,0:T(8,128)(2,1)S(1)} %bitcast.105), channel_id=1, source_target_pairs={{0,225},{1,224},{32,1},{33,0},{64,33},{65,32},{96,65},{97,64},{128... | collective-permute-start | bytes 1179656 | tf_op jit(solution)/shard_map/ppermute | solution.py:192
  8.5 3.2 %collective-permute-start = (bf16[192,1024]{1,0:T(8,128)(2,1)S(1)}, bf16[192,1024]{1,0:T(8,128)(2,1)S(1)}, u32[]{:S(2)}, u32[]{:S(2)}) collective-permute-start(bf16[192,1024]{1,0:T(8,128)(2,1)S(1)} %bitcast.99), channel_id=1, source_target_pairs={{0,224},{32,0},{64,32},{96,64},{128,96},{160,128},{192,160},{224,1... | collective-permute-start | bytes 1179656 | tf_op jit(solution)/shard_map/ppermute | solution.py:194
  11.8 5.0 %collective-permute-done.2.refs_7_ = bf16[192,1024]{1,0:T(8,128)(2,1)S(1)} collective-permute-done((bf16[192,1024]{1,0:T(8,128)(2,1)S(1)}, bf16[192,1024]{1,0:T(8,128)(2,1)S(1)}, u32[]{:S(2)}, u32[]{:S(2)}) %collective-permute-start.2) | collective-permute-done | bytes 393248 | tf_op jit(solution)/shard_map/ppermute | solution.py:192
  20.4 6.5 %collective-permute-done.11.refs_3_ = bf16[192,1024]{1,0:T(8,128)(2,1)S(1)} collective-permute-done((bf16[192,1024]{1,0:T(8,128)(2,1)S(1)}, bf16[192,1024]{1,0:T(8,128)(2,1)S(1)}, u32[]{:S(2)}, u32[]{:S(2)}) %collective-permute-start.11) | collective-permute-done | bytes 393248 | tf_op jit(solution)/shard_map/ppermute | solution.py:192
  26.9 3.2 %collective-permute-start.1 = (bf16[192,1024]{1,0:T(8,128)(2,1)S(1)}, bf16[192,1024]{1,0:T(8,128)(2,1)S(1)}, u32[]{:S(2)}, u32[]{:S(2)}) collective-permute-start(bf16[192,1024]{1,0:T(8,128)(2,1)S(1)} %collective-permute-done.refs_6_), channel_id=1, source_target_pairs={{0,224},{32,0},{64,32},{96,64},{128,96},{160,128},{192,160},{224,1... | collective-permute-start | bytes 1179656 | tf_op jit(solution)/shard_map/ppermute | solution.py:194
  30.2 3.4 %collective-permute-done.3.refs_1_ = bf16[192,1024]{1,0:T(8,128)(2,1)S(1)} collective-permute-done((bf16[192,1024]{1,0:T(8,128)(2,1)S(1)}, bf16[192,1024]{1,0:T(8,128)(2,1)S(1)}, u32[]{:S(2)}, u32[]{:S(2)}) %collective-permute-start.3) | collective-permute-done | bytes 393248 | tf_op jit(solution)/shard_map/ppermute | solution.py:194
  33.6 3.7 %collective-permute-start.5 = (bf16[192,1024]{1,0:T(8,128)(2,1)S(1)}, bf16[192,1024]{1,0:T(8,128)(2,1)S(1)}, u32[]{:S(2)}, u32[]{:S(2)}) collective-permute-start(bf16[192,1024]{1,0:T(8,128)(2,1)S(1)} %collective-permute-done.3.refs_1_), channel_id=1, source_target_pairs={{0,224},{32,0},{64,32},{96,64},{128,96},{160,128},{192,160},{224,1... | collective-permute-start | bytes 1179656 | tf_op jit(solution)/shard_map/ppermute | solution.py:194
  38.2 7.5 %collective-permute-done.12.refs_1_ = bf16[192,1024]{1,0:T(8,128)(2,1)S(1)} collective-permute-done((bf16[192,1024]{1,0:T(8,128)(2,1)S(1)}, bf16[192,1024]{1,0:T(8,128)(2,1)S(1)}, u32[]{:S(2)}, u32[]{:S(2)}) %collective-permute-start.12) | collective-permute-done | bytes 393248 | tf_op jit(solution)/shard_map/ppermute | solution.py:194
  45.7 4.0 %collective-permute-done.5.refs_3_ = bf16[192,1024]{1,0:T(8,128)(2,1)S(1)} collective-permute-done((bf16[192,1024]{1,0:T(8,128)(2,1)S(1)}, bf16[192,1024]{1,0:T(8,128)(2,1)S(1)}, u32[]{:S(2)}, u32[]{:S(2)}) %collective-permute-start.5) | collective-permute-done | bytes 393248 | tf_op jit(solution)/shard_map/ppermute | solution.py:194
  49.8 3.7 %collective-permute-start.4 = (bf16[192,1024]{1,0:T(8,128)(2,1)S(1)}, bf16[192,1024]{1,0:T(8,128)(2,1)S(1)}, u32[]{:S(2)}, u32[]{:S(2)}) collective-permute-start(bf16[192,1024]{1,0:T(8,128)(2,1)S(1)} %collective-permute-done.1.refs_0_), channel_id=1, source_target_pairs={{0,224},{32,0},{64,32},{96,64},{128,96},{160,128},{192,160},{224,1... | collective-permute-start | bytes 1179656 | tf_op jit(solution)/shard_map/ppermute | solution.py:194
  56.2 2.9 %compare_select_fusion = (bf16[1024,1024]{1,0:T(8,128)(2,1)S(1)}, bf16[1024,1024]{1,0:T(8,128)(2,1)S(1)}) fusion(bf16[1024,1024]{1,0:T(8,128)(2,1)} %collective-permute-done.15, s32[1024]{0:T(1024)S(1)} %broadcast_bitcast_fusion, s32[1024]{0:T(1024)S(1)} %get-tuple-element.40, bf16[1024,1024]{1,0:T(8,128)(2,1)} %param.6, s32[1024]{0:T(1024)S(1)} %get-tuple-element.39), kind=kLoop, calls=%fused_computation | loop fusion | flops 4194304 | bytes 8400896 | tf_op jit(solution)/shard_map/jit(_where)/select_n | solution.py:165
  64.1 6.2 %shard_map.55 = (f32[8,96,1024]{2,1,0:T(8,128)S(1)}, f32[8,96,1024]{2,1,0:T(8,128)}) custom-call(bf16[192,1024]{1,0:T(8,128)(2,1)S(1)} %copy-done.11, bf16[192,1024]{1,0:T(8,128)(2,1)S(1)} %collective-permute-done.12.refs_1_, bf16[192,1024]{1,0:T(8,128)(2,1)S(1)} %copy-done.5, bf16[192,1024]{1,0:T(8,128)(2,1)S(1)} %copy-done.7, ...), custom_call_target="tpu_custom_call" | custom-call | flops 3221225472 | bytes 10485760 | tf_op jit(solution)/shard_map/pallas_call | solution.py:97
  70.3 6.1 %shard_map.56 = (f32[8,96,1024]{2,1,0:T(8,128)S(1)}, f32[8,96,1024]{2,1,0:T(8,128)}) custom-call(bf16[192,1024]{1,0:T(8,128)(2,1)S(1)} %collective-permute-done.1.refs_0_, bf16[192,1024]{1,0:T(8,128)(2,1)S(1)} %copy-done.1, bf16[192,1024]{1,0:T(8,128)(2,1)S(1)} %collective-permute-done.4.refs_2_, ...), custom_call_target="tpu_custom_call", output_to_operand_aliasing={{0}: (10, {}), {1}: (11, {})} | custom-call | flops 3221225472 | bytes 10485760 | tf_op jit(solution)/shard_map/pallas_call | solution.py:97
  79.7 2.9 %dynamic-slice_bitcast_fusion.8 = (f32[2,48,1024]{2,1,0:T(8,128)}, f32[2,48,1024]{2,1,0:T(8,128)}, f32[2,48,1024]{2,1,0:T(8,128)}, f32[2,48,1024]{2,1,0:T(8,128)...) fusion(f32[8,2,48,1024]{3,2,1,0:T(8,128)} %bitcast.102, s32[]{:T(128)S(6)} %select_n.280, s32[]{:T(128)S(6)} %select_n.286, ...), kind=kLoop, calls=%fused_computation.19 | loop fusion | bytes 4718616 | tf_op jit(solution)/shard_map/jit(dynamic_index_in_dim)/squeeze | solution.py:24
  93.4 3.6 %collective-permute-start.29 = (f32[2,48,1024]{2,1,0:T(8,128)}, f32[2,48,1024]{2,1,0:T(8,128)}, u32[]{:S(2)}, u32[]{:S(2)}) collective-permute-start(f32[2,48,1024]{2,1,0:T(8,128)} %get-tuple-element.19), channel_id=1, source_target_pairs={{0,24},{8,0},{16,8},{24,16},{1,25},{9,1},{17,9},{25,17},{2,26},{10... | collective-permute-start | bytes 1179656 | tf_op jit(solution)/shard_map/ppermute | solution.py:41
  98.8 2.4 %bitcast_add_fusion.2 = (f32[2,48,1024]{2,1,0:T(8,128)}, f32[2,48,1024]{2,1,0:T(8,128)}) fusion(f32[2,48,1024]{2,1,0:T(8,128)} %collective-permute-done.27, f32[8,2,48,1024]{3,2,1,0:T(8,128)} %bitcast.103, s32[]{:T(128)S(6)} %select_n.276, f32[2,48,1024]{2,1,0:T(8,128)} %collective-permute-done.30, s32[]{:T(128)S(6)} %select_n.282), kind=kLoop, calls=%fused_computation.16 | loop fusion | flops 196608 | bytes 2359304 | tf_op jit(solution)/shard_map/add | solution.py:42
  105.6 3.0 %collective-permute-start.31 = (f32[2,48,1024]{2,1,0:T(8,128)}, f32[2,48,1024]{2,1,0:T(8,128)}, u32[]{:S(2)}, u32[]{:S(2)}) collective-permute-start(f32[2,48,1024]{2,1,0:T(8,128)} %get-tuple-element.26), channel_id=1, source_target_pairs={{0,24},{8,0},{16,8},{24,16},{1,25},{9,1},{17,9},{25,17},{2,26},{10... | collective-permute-start | bytes 1179656 | tf_op jit(solution)/shard_map/ppermute | solution.py:43
  111.2 3.2 %collective-permute-start.25 = (f32[24,1024]{1,0:T(8,128)S(1)}, f32[24,1024]{1,0:T(8,128)S(1)}, u32[]{:S(2)}, u32[]{:S(2)}) collective-permute-start(f32[24,1024]{1,0:T(8,128)S(1)} %get-tuple-element.30), channel_id=1, source_target_pairs={{0,24},{8,0},{16,8},{24,16},{1,25},{9,1},{17,9},{25,17},{2,26},{10... | collective-permute-start | bytes 294920 | tf_op jit(solution)/shard_map/ppermute | solution.py:34
  114.4 3.7 %collective-permute-done.28 = f32[2,48,1024]{2,1,0:T(8,128)} collective-permute-done((f32[2,48,1024]{2,1,0:T(8,128)}, f32[2,48,1024]{2,1,0:T(8,128)}, u32[]{:S(2)}, u32[]{:S(2)}) %collective-permute-start.28) | collective-permute-done | bytes 393248 | tf_op jit(solution)/shard_map/ppermute | solution.py:42
  122.9 3.2 %collective-permute-start.26 = (f32[48,1024]{1,0:T(8,128)S(1)}, f32[48,1024]{1,0:T(8,128)S(1)}, u32[]{:S(2)}, u32[]{:S(2)}) collective-permute-start(f32[48,1024]{1,0:T(8,128)S(1)} %get-tuple-element.28), channel_id=1, source_target_pairs={{0,24},{8,0},{16,8},{24,16},{1,25},{9,1},{17,9},{25,17},{2,26},{10... | collective-permute-start | bytes 589832 | tf_op jit(solution)/shard_map/ppermute | solution.py:38
  131.6 2.7 %collective-permute-done.34 = f32[48,1024]{1,0:T(8,128)S(1)} collective-permute-done((f32[48,1024]{1,0:T(8,128)S(1)}, f32[48,1024]{1,0:T(8,128)S(1)}, u32[]{:S(2)}, u32[]{:S(2)}) %collective-permute-start.34) | collective-permute-done | bytes 196640 | tf_op jit(solution)/shard_map/ppermute | solution.py:37
  136.8 3.9 %all-to-all-start = ((f32[8,12,1024]{2,1,0:T(8,128)}), f32[8,12,1024]{2,1,0:T(8,128)S(1)}, u32[]{:S(2)}, u32[]{:S(2)}) async-start(f32[8,12,1024]{2,1,0:T(8,128)} %reshape.57), calls=%async_computation | async-start | bytes 1048576 | tf_op jit(solution)/shard_map/all_to_all | solution.py:223
  140.9 13.3 %all-to-all-done.given_ref = f32[8,12,1024]{2,1,0:T(8,128)S(1)} async-done(((f32[8,12,1024]{2,1,0:T(8,128)}), f32[8,12,1024]{2,1,0:T(8,128)S(1)}, u32[]{:S(2)}, u32[]{:S(2)}) %all-to-all-start) | async-done | bytes 393248 | tf_op jit(solution)/shard_map/all_to_all | solution.py:223
  155.3 12.9 %all_to_all.10 = bf16[8,12,1024]{2,1,0:T(8,128)(2,1)S(1)} all-to-all(bf16[8,12,1024]{2,1,0:T(8,128)(2,1)S(1)} %shard_map.57), channel_id=1, replica_groups=mesh['z'=8,'y'=4,'x'=4,'c'=2] {'z'}, dimensions={0} | all-to-all | bytes 393216 | tf_op jit(solution)/shard_map/all_to_all | solution.py:225
  (112 shorter events, 52.2 us)
Async XLA Ops:
  0.0 54.1 %collective-permute-start.15 = (bf16[1024,1024]{1,0:T(8,128)(2,1)}, bf16[1024,1024]{1,0:T(8,128)(2,1)}, u32[]{:S(2)}, u32[]{:S(2)}) collective-permute-start(bf16[1024,1024]{1,0:T(8,128)(2,1)} %param.6), channel_id=1, source_target_pairs={{0,1},{1,0},{2,3},{3,2},{4,5},{5,4},{6,7},{7,6},{8,9},{9,8},{10,11... | collective-permute-start | bytes 6291464 | tf_op jit(solution)/shard_map/ppermute | solution.py:168
  1.2 15.6 %collective-permute-start.2 = (bf16[192,1024]{1,0:T(8,128)(2,1)S(1)}, bf16[192,1024]{1,0:T(8,128)(2,1)S(1)}, u32[]{:S(2)}, u32[]{:S(2)}) collective-permute-start(bf16[192,1024]{1,0:T(8,128)(2,1)S(1)} %bitcast.105), channel_id=1, source_target_pairs={{0,225},{1,224},{32,1},{33,0},{64,33},{65,32},{96,65},{97,64},{128... | collective-permute-start | bytes 1179656 | tf_op jit(solution)/shard_map/ppermute | solution.py:192
  7.2 13.2 %collective-permute-start.6 = (bf16[192,1024]{1,0:T(8,128)(2,1)S(1)}, bf16[192,1024]{1,0:T(8,128)(2,1)S(1)}, u32[]{:S(2)}, u32[]{:S(2)}) collective-permute-start(bf16[192,1024]{1,0:T(8,128)(2,1)S(1)} %bitcast.98), channel_id=1, source_target_pairs={{0,32},{32,64},{64,96},{96,128},{128,160},{160,192},{192,224},{224... | collective-permute-start | bytes 1179656 | tf_op jit(solution)/shard_map/ppermute | solution.py:194
  7.2 19.7 %collective-permute-start.11 = (bf16[192,1024]{1,0:T(8,128)(2,1)S(1)}, bf16[192,1024]{1,0:T(8,128)(2,1)S(1)}, u32[]{:S(2)}, u32[]{:S(2)}) collective-permute-start(bf16[192,1024]{1,0:T(8,128)(2,1)S(1)} %bitcast.106), channel_id=1, source_target_pairs={{0,33},{1,32},{32,65},{33,64},{64,97},{65,96},{96,129},{97,128},{1... | collective-permute-start | bytes 1179656 | tf_op jit(solution)/shard_map/ppermute | solution.py:192
  8.5 18.4 %collective-permute-start = (bf16[192,1024]{1,0:T(8,128)(2,1)S(1)}, bf16[192,1024]{1,0:T(8,128)(2,1)S(1)}, u32[]{:S(2)}, u32[]{:S(2)}) collective-permute-start(bf16[192,1024]{1,0:T(8,128)(2,1)S(1)} %bitcast.99), channel_id=1, source_target_pairs={{0,224},{32,0},{64,32},{96,64},{128,96},{160,128},{192,160},{224,1... | collective-permute-start | bytes 1179656 | tf_op jit(solution)/shard_map/ppermute | solution.py:194
  16.7 16.9 %collective-permute-start.3 = (bf16[192,1024]{1,0:T(8,128)(2,1)S(1)}, bf16[192,1024]{1,0:T(8,128)(2,1)S(1)}, u32[]{:S(2)}, u32[]{:S(2)}) collective-permute-start(bf16[192,1024]{1,0:T(8,128)(2,1)S(1)} %collective-permute-done.2.refs_7_), channel_id=1, source_target_pairs={{0,224},{32,0},{64,32},{96,64},{128,96},{160,128},{192,160},{224,1... | collective-permute-start | bytes 1179656 | tf_op jit(solution)/shard_map/ppermute | solution.py:194
  20.4 16.9 %collective-permute-start.7 = (bf16[192,1024]{1,0:T(8,128)(2,1)S(1)}, bf16[192,1024]{1,0:T(8,128)(2,1)S(1)}, u32[]{:S(2)}, u32[]{:S(2)}) collective-permute-start(bf16[192,1024]{1,0:T(8,128)(2,1)S(1)} %collective-permute-done.6.refs_2_), channel_id=1, source_target_pairs={{0,32},{32,64},{64,96},{96,128},{128,160},{160,192},{192,224},{224... | collective-permute-start | bytes 1179656 | tf_op jit(solution)/shard_map/ppermute | solution.py:194
  26.9 18.8 %collective-permute-start.12 = (bf16[192,1024]{1,0:T(8,128)(2,1)S(1)}, bf16[192,1024]{1,0:T(8,128)(2,1)S(1)}, u32[]{:S(2)}, u32[]{:S(2)}) collective-permute-start(bf16[192,1024]{1,0:T(8,128)(2,1)S(1)} %collective-permute-done.11.refs_3_), channel_id=1, source_target_pairs={{0,32},{32,64},{64,96},{96,128},{128,160},{160,192},{192,224},{224... | collective-permute-start | bytes 1179656 | tf_op jit(solution)/shard_map/ppermute | solution.py:194
  26.9 18.8 %collective-permute-start.1 = (bf16[192,1024]{1,0:T(8,128)(2,1)S(1)}, bf16[192,1024]{1,0:T(8,128)(2,1)S(1)}, u32[]{:S(2)}, u32[]{:S(2)}) collective-permute-start(bf16[192,1024]{1,0:T(8,128)(2,1)S(1)} %collective-permute-done.refs_6_), channel_id=1, source_target_pairs={{0,224},{32,0},{64,32},{96,64},{128,96},{160,128},{192,160},{224,1... | collective-permute-start | bytes 1179656 | tf_op jit(solution)/shard_map/ppermute | solution.py:194
  33.6 16.2 %collective-permute-start.5 = (bf16[192,1024]{1,0:T(8,128)(2,1)S(1)}, bf16[192,1024]{1,0:T(8,128)(2,1)S(1)}, u32[]{:S(2)}, u32[]{:S(2)}) collective-permute-start(bf16[192,1024]{1,0:T(8,128)(2,1)S(1)} %collective-permute-done.3.refs_1_), channel_id=1, source_target_pairs={{0,224},{32,0},{64,32},{96,64},{128,96},{160,128},{192,160},{224,1... | collective-permute-start | bytes 1179656 | tf_op jit(solution)/shard_map/ppermute | solution.py:194
  37.3 16.8 %collective-permute-start.8 = (bf16[192,1024]{1,0:T(8,128)(2,1)S(1)}, bf16[192,1024]{1,0:T(8,128)(2,1)S(1)}, u32[]{:S(2)}, u32[]{:S(2)}) collective-permute-start(bf16[192,1024]{1,0:T(8,128)(2,1)S(1)} %collective-permute-done.7.refs_0_), channel_id=1, source_target_pairs={{0,32},{32,64},{64,96},{96,128},{128,160},{160,192},{192,224},{224... | collective-permute-start | bytes 1179656 | tf_op jit(solution)/shard_map/ppermute | solution.py:194
  45.7 13.4 %collective-permute-start.16 = (bf16[2,96,1024]{2,1,0:T(8,128)(2,1)S(1)}, bf16[2,96,1024]{2,1,0:T(8,128)(2,1)S(1)}, u32[]{:S(2)}, u32[]{:S(2)}) collective-permute-start(bf16[2,96,1024]{2,1,0:T(8,128)(2,1)S(1)} %bitcast.107), channel_id=1, source_target_pairs={{0,1},{1,0},{2,3},{3,2},{4,5},{5,4},{6,7},{7,6},{8,9},{9,8},{10,11... | collective-permute-start | bytes 1179656 | tf_op jit(solution)/shard_map/ppermute | solution.py:174
  45.7 24.6 %collective-permute-start.13 = (bf16[192,1024]{1,0:T(8,128)(2,1)S(1)}, bf16[192,1024]{1,0:T(8,128)(2,1)S(1)}, u32[]{:S(2)}, u32[]{:S(2)}) collective-permute-start(bf16[192,1024]{1,0:T(8,128)(2,1)S(1)} %collective-permute-done.12.refs_1_), channel_id=1, source_target_pairs={{0,32},{32,64},{64,96},{96,128},{128,160},{160,192},{192,224},{224... | collective-permute-start | bytes 1179656 | tf_op jit(solution)/shard_map/ppermute | solution.py:194
  49.8 20.5 %collective-permute-start.4 = (bf16[192,1024]{1,0:T(8,128)(2,1)S(1)}, bf16[192,1024]{1,0:T(8,128)(2,1)S(1)}, u32[]{:S(2)}, u32[]{:S(2)}) collective-permute-start(bf16[192,1024]{1,0:T(8,128)(2,1)S(1)} %collective-permute-done.1.refs_0_), channel_id=1, source_target_pairs={{0,224},{32,0},{64,32},{96,64},{128,96},{160,128},{192,160},{224,1... | collective-permute-start | bytes 1179656 | tf_op jit(solution)/shard_map/ppermute | solution.py:194
  54.1 16.2 %collective-permute-start.10 = (bf16[192,1024]{1,0:T(8,128)(2,1)S(1)}, bf16[192,1024]{1,0:T(8,128)(2,1)S(1)}, u32[]{:S(2)}, u32[]{:S(2)}) collective-permute-start(bf16[192,1024]{1,0:T(8,128)(2,1)S(1)} %collective-permute-done.5.refs_3_), channel_id=1, source_target_pairs={{0,224},{32,0},{64,32},{96,64},{128,96},{160,128},{192,160},{224,1... | collective-permute-start | bytes 1179656 | tf_op jit(solution)/shard_map/ppermute | solution.py:194
  54.1 16.2 %collective-permute-start.9 = (bf16[192,1024]{1,0:T(8,128)(2,1)S(1)}, bf16[192,1024]{1,0:T(8,128)(2,1)S(1)}, u32[]{:S(2)}, u32[]{:S(2)}) collective-permute-start(bf16[192,1024]{1,0:T(8,128)(2,1)S(1)} %collective-permute-done.8.refs_6_), channel_id=1, source_target_pairs={{0,32},{32,64},{64,96},{96,128},{128,160},{160,192},{192,224},{224... | collective-permute-start | bytes 1179656 | tf_op jit(solution)/shard_map/ppermute | solution.py:194
  84.1 12.9 %collective-permute-start.30 = (f32[2,48,1024]{2,1,0:T(8,128)}, f32[2,48,1024]{2,1,0:T(8,128)}, u32[]{:S(2)}, u32[]{:S(2)}) collective-permute-start(f32[2,48,1024]{2,1,0:T(8,128)} %get-tuple-element.21), channel_id=1, source_target_pairs={{0,24},{8,0},{16,8},{24,16},{1,25},{9,1},{17,9},{25,17},{2,26},{10... | collective-permute-start | bytes 1179656 | tf_op jit(solution)/shard_map/ppermute | solution.py:34
  85.8 15.4 %collective-permute-start.19 = (f32[2,48,1024]{2,1,0:T(8,128)}, f32[2,48,1024]{2,1,0:T(8,128)}, u32[]{:S(2)}, u32[]{:S(2)}) collective-permute-start(f32[2,48,1024]{2,1,0:T(8,128)} %get-tuple-element.13), channel_id=1, source_target_pairs={{0,6},{2,0},{4,2},{6,4},{1,7},{3,1},{5,3},{7,5},{8,14},{10,8},{12,... | collective-permute-start | bytes 1179656 | tf_op jit(solution)/shard_map/ppermute | solution.py:41
  87.8 13.8 %collective-permute-start.22 = (f32[2,48,1024]{2,1,0:T(8,128)}, f32[2,48,1024]{2,1,0:T(8,128)}, u32[]{:S(2)}, u32[]{:S(2)}) collective-permute-start(f32[2,48,1024]{2,1,0:T(8,128)} %get-tuple-element.16), channel_id=1, source_target_pairs={{0,2},{2,4},{4,6},{6,0},{1,3},{3,5},{5,7},{7,1},{8,10},{10,12},{12... | collective-permute-start | bytes 1179656 | tf_op jit(solution)/shard_map/ppermute | solution.py:40
  93.4 17.8 %collective-permute-start.29 = (f32[2,48,1024]{2,1,0:T(8,128)}, f32[2,48,1024]{2,1,0:T(8,128)}, u32[]{:S(2)}, u32[]{:S(2)}) collective-permute-start(f32[2,48,1024]{2,1,0:T(8,128)} %get-tuple-element.19), channel_id=1, source_target_pairs={{0,24},{8,0},{16,8},{24,16},{1,25},{9,1},{17,9},{25,17},{2,26},{10... | collective-permute-start | bytes 1179656 | tf_op jit(solution)/shard_map/ppermute | solution.py:41
  101.2 18.1 %collective-permute-start.32 = (f32[2,48,1024]{2,1,0:T(8,128)}, f32[2,48,1024]{2,1,0:T(8,128)}, u32[]{:S(2)}, u32[]{:S(2)}) collective-permute-start(f32[2,48,1024]{2,1,0:T(8,128)} %get-tuple-element.20), channel_id=1, source_target_pairs={{0,8},{8,16},{16,24},{24,0},{1,9},{9,17},{17,25},{25,1},{2,10},{10... | collective-permute-start | bytes 1179656 | tf_op jit(solution)/shard_map/ppermute | solution.py:40
  101.6 16.5 %collective-permute-start.28 = (f32[2,48,1024]{2,1,0:T(8,128)}, f32[2,48,1024]{2,1,0:T(8,128)}, u32[]{:S(2)}, u32[]{:S(2)}) collective-permute-start(f32[2,48,1024]{2,1,0:T(8,128)} %get-tuple-element.25), channel_id=1, source_target_pairs={{0,8},{8,16},{16,24},{24,0},{1,9},{9,17},{17,25},{25,1},{2,10},{10... | collective-permute-start | bytes 1179656 | tf_op jit(solution)/shard_map/ppermute | solution.py:42
  105.6 13.8 %collective-permute-start.31 = (f32[2,48,1024]{2,1,0:T(8,128)}, f32[2,48,1024]{2,1,0:T(8,128)}, u32[]{:S(2)}, u32[]{:S(2)}) collective-permute-start(f32[2,48,1024]{2,1,0:T(8,128)} %get-tuple-element.26), channel_id=1, source_target_pairs={{0,24},{8,0},{16,8},{24,16},{1,25},{9,1},{17,9},{25,17},{2,26},{10... | collective-permute-start | bytes 1179656 | tf_op jit(solution)/shard_map/ppermute | solution.py:43
  136.8 17.4 %all-to-all-start = ((f32[8,12,1024]{2,1,0:T(8,128)}), f32[8,12,1024]{2,1,0:T(8,128)S(1)}, u32[]{:S(2)}, u32[]{:S(2)}) async-start(f32[8,12,1024]{2,1,0:T(8,128)} %reshape.57), calls=%async_computation | async-start | bytes 1048576 | tf_op jit(solution)/shard_map/all_to_all | solution.py:223
  (29 other events, 368.4 us)

commit v2 on v1

--- a/solution.py
+++ b/solution.py
@@ -220,9 +220,10 @@
     sums = jnp.concatenate([first, second], axis=0)
 
     share = rows // levels
-    spread = lax.all_to_all(sums.reshape(levels, share, ab), "z", 0, 0)
-    result = antisymmetrize(spread, mirror_rows)
-    return lax.all_to_all(result, "z", 0, 0).reshape(rows, ab)
+    grouped = (levels, share // 4, 4, ab)
+    spread = lax.all_to_all(sums.reshape(grouped), "z", 0, 0)
+    result = antisymmetrize(spread.reshape(levels, share, ab), mirror_rows)
+    return lax.all_to_all(result.reshape(grouped), "z", 0, 0).reshape(rows, ab)
 
 
 def solution(mesh):

time: 170 us -> 168 us (0.988)
  no operation moved by 1% of the time
where the time goes in v2:
time: 168 us
  starting transfers between devices  57.3 us (34%)
  waiting for transfers between devices  57.3 us (34%)
  local copies, waits for them, and re-layouts  13.6 us (8%)
  other arithmetic  13.4 us (8%)
  Pallas kernels  13.4 us (8%)
  blocking collectives  12.2 us (7%)
    ppermute x12, starting transfers between devices, shards(): got = lax.ppermute(moving[h, d], 'z', shift(levels, d))  18.2 us
    ppermute x12, waiting for transfers between devices, shards(): got = lax.ppermute(moving[h, d], 'z', shift(levels, d))  17.1 us
    pallas_call x2, Pallas kernels, product(): pl.pallas_call(functools.partial(product_kernel, size, count), grid=(1,),...  12.3 us
    all_to_all x1, blocking collectives, shards(): return lax.all_to_all(result.reshape(grouped), 'z', 0, 0).reshape(rows, ab)  12.2 us
    all_to_all x1, waiting for transfers between devices, shards(): spread = lax.all_to_all(sums.reshape(grouped), 'z', 0, 0)  11.9 us
    ppermute x2, waiting for transfers between devices, shards(): got = lax.ppermute(moving[h, d], ('z', 'c'), cross(levels, d))  11.5 us
    ppermute x4, starting transfers between devices, scatter_ring(): from_down = send_down(far[half:])  6.89 us
    ppermute x2, waiting for transfers between devices, scatter_ring(): up = send_up(up[:half] + from_up)  6.06 us
  transfers between devices with their start and end apart: 38, of which 18 were waited for; matrix products, arithmetic and copies ran while one was open for 11% of the time, Pallas kernels for 4%

profile of v2, /device:TPU:6, one launch (start us, length us, event | category | flops | bytes accessed | tf_op | source)
XLA Modules:
  0.0 167.6 jit_solution(11165006190914632941)
XLA Ops:
  1.2 6.0 %collective-permute-start.2 = (bf16[192,1024]{1,0:T(8,128)(2,1)S(1)}, bf16[192,1024]{1,0:T(8,128)(2,1)S(1)}, u32[]{:S(2)}, u32[]{:S(2)}) collective-permute-start(bf16[192,1024]{1,0:T(8,128)(2,1)S(1)} %bitcast.109), channel_id=1, source_target_pairs={{0,225},{1,224},{32,1},{33,0},{64,33},{65,32},{96,65},{97,64},{128... | collective-permute-start | bytes 1179656 | tf_op jit(solution)/shard_map/ppermute | solution.py:192
  8.5 3.2 %collective-permute-start = (bf16[192,1024]{1,0:T(8,128)(2,1)S(1)}, bf16[192,1024]{1,0:T(8,128)(2,1)S(1)}, u32[]{:S(2)}, u32[]{:S(2)}) collective-permute-start(bf16[192,1024]{1,0:T(8,128)(2,1)S(1)} %bitcast.101), channel_id=1, source_target_pairs={{0,224},{32,0},{64,32},{96,64},{128,96},{160,128},{192,160},{224,1... | collective-permute-start | bytes 1179656 | tf_op jit(solution)/shard_map/ppermute | solution.py:194
  11.8 5.0 %collective-permute-done.2.refs_7_ = bf16[192,1024]{1,0:T(8,128)(2,1)S(1)} collective-permute-done((bf16[192,1024]{1,0:T(8,128)(2,1)S(1)}, bf16[192,1024]{1,0:T(8,128)(2,1)S(1)}, u32[]{:S(2)}, u32[]{:S(2)}) %collective-permute-start.2) | collective-permute-done | bytes 393248 | tf_op jit(solution)/shard_map/ppermute | solution.py:192
  20.4 6.5 %collective-permute-done.11.refs_3_ = bf16[192,1024]{1,0:T(8,128)(2,1)S(1)} collective-permute-done((bf16[192,1024]{1,0:T(8,128)(2,1)S(1)}, bf16[192,1024]{1,0:T(8,128)(2,1)S(1)}, u32[]{:S(2)}, u32[]{:S(2)}) %collective-permute-start.11) | collective-permute-done | bytes 393248 | tf_op jit(solution)/shard_map/ppermute | solution.py:192
  26.9 3.2 %collective-permute-start.1 = (bf16[192,1024]{1,0:T(8,128)(2,1)S(1)}, bf16[192,1024]{1,0:T(8,128)(2,1)S(1)}, u32[]{:S(2)}, u32[]{:S(2)}) collective-permute-start(bf16[192,1024]{1,0:T(8,128)(2,1)S(1)} %collective-permute-done.refs_6_), channel_id=1, source_target_pairs={{0,224},{32,0},{64,32},{96,64},{128,96},{160,128},{192,160},{224,1... | collective-permute-start | bytes 1179656 | tf_op jit(solution)/shard_map/ppermute | solution.py:194
  30.2 3.4 %collective-permute-done.3.refs_1_ = bf16[192,1024]{1,0:T(8,128)(2,1)S(1)} collective-permute-done((bf16[192,1024]{1,0:T(8,128)(2,1)S(1)}, bf16[192,1024]{1,0:T(8,128)(2,1)S(1)}, u32[]{:S(2)}, u32[]{:S(2)}) %collective-permute-start.3) | collective-permute-done | bytes 393248 | tf_op jit(solution)/shard_map/ppermute | solution.py:194
  33.6 3.7 %collective-permute-start.5 = (bf16[192,1024]{1,0:T(8,128)(2,1)S(1)}, bf16[192,1024]{1,0:T(8,128)(2,1)S(1)}, u32[]{:S(2)}, u32[]{:S(2)}) collective-permute-start(bf16[192,1024]{1,0:T(8,128)(2,1)S(1)} %collective-permute-done.3.refs_1_), channel_id=1, source_target_pairs={{0,224},{32,0},{64,32},{96,64},{128,96},{160,128},{192,160},{224,1... | collective-permute-start | bytes 1179656 | tf_op jit(solution)/shard_map/ppermute | solution.py:194
  38.2 7.5 %collective-permute-done.12.refs_1_ = bf16[192,1024]{1,0:T(8,128)(2,1)S(1)} collective-permute-done((bf16[192,1024]{1,0:T(8,128)(2,1)S(1)}, bf16[192,1024]{1,0:T(8,128)(2,1)S(1)}, u32[]{:S(2)}, u32[]{:S(2)}) %collective-permute-start.12) | collective-permute-done | bytes 393248 | tf_op jit(solution)/shard_map/ppermute | solution.py:194
  45.7 4.0 %collective-permute-done.5.refs_3_ = bf16[192,1024]{1,0:T(8,128)(2,1)S(1)} collective-permute-done((bf16[192,1024]{1,0:T(8,128)(2,1)S(1)}, bf16[192,1024]{1,0:T(8,128)(2,1)S(1)}, u32[]{:S(2)}, u32[]{:S(2)}) %collective-permute-start.5) | collective-permute-done | bytes 393248 | tf_op jit(solution)/shard_map/ppermute | solution.py:194
  49.8 3.7 %collective-permute-start.4 = (bf16[192,1024]{1,0:T(8,128)(2,1)S(1)}, bf16[192,1024]{1,0:T(8,128)(2,1)S(1)}, u32[]{:S(2)}, u32[]{:S(2)}) collective-permute-start(bf16[192,1024]{1,0:T(8,128)(2,1)S(1)} %collective-permute-done.1.refs_0_), channel_id=1, source_target_pairs={{0,224},{32,0},{64,32},{96,64},{128,96},{160,128},{192,160},{224,1... | collective-permute-start | bytes 1179656 | tf_op jit(solution)/shard_map/ppermute | solution.py:194
  56.2 2.9 %compare_select_fusion = (bf16[1024,1024]{1,0:T(8,128)(2,1)S(1)}, bf16[1024,1024]{1,0:T(8,128)(2,1)S(1)}) fusion(bf16[1024,1024]{1,0:T(8,128)(2,1)} %collective-permute-done.15, s32[1024]{0:T(1024)S(1)} %broadcast_bitcast_fusion, s32[1024]{0:T(1024)S(1)} %get-tuple-element.40, bf16[1024,1024]{1,0:T(8,128)(2,1)} %param.6, s32[1024]{0:T(1024)S(1)} %get-tuple-element.39), kind=kLoop, calls=%fused_computation | loop fusion | flops 4194304 | bytes 8400896 | tf_op jit(solution)/shard_map/jit(_where)/select_n | solution.py:165
  64.1 6.2 %shard_map.55 = (f32[8,96,1024]{2,1,0:T(8,128)S(1)}, f32[8,96,1024]{2,1,0:T(8,128)}) custom-call(bf16[192,1024]{1,0:T(8,128)(2,1)S(1)} %copy-done.11, bf16[192,1024]{1,0:T(8,128)(2,1)S(1)} %collective-permute-done.12.refs_1_, bf16[192,1024]{1,0:T(8,128)(2,1)S(1)} %copy-done.5, bf16[192,1024]{1,0:T(8,128)(2,1)S(1)} %copy-done.7, ...), custom_call_target="tpu_custom_call" | custom-call | flops 3221225472 | bytes 10485760 | tf_op jit(solution)/shard_map/pallas_call | solution.py:97
  70.3 6.1 %shard_map.56 = (f32[8,96,1024]{2,1,0:T(8,128)S(1)}, f32[8,96,1024]{2,1,0:T(8,128)}) custom-call(bf16[192,1024]{1,0:T(8,128)(2,1)S(1)} %collective-permute-done.1.refs_0_, bf16[192,1024]{1,0:T(8,128)(2,1)S(1)} %copy-done.1, bf16[192,1024]{1,0:T(8,128)(2,1)S(1)} %collective-permute-done.4.refs_2_, ...), custom_call_target="tpu_custom_call", output_to_operand_aliasing={{0}: (10, {}), {1}: (11, {})} | custom-call | flops 3221225472 | bytes 10485760 | tf_op jit(solution)/shard_map/pallas_call | solution.py:97
  79.7 2.9 %dynamic-slice_bitcast_fusion.8 = (f32[2,48,1024]{2,1,0:T(8,128)}, f32[2,48,1024]{2,1,0:T(8,128)}, f32[2,48,1024]{2,1,0:T(8,128)}, f32[2,48,1024]{2,1,0:T(8,128)...) fusion(f32[8,2,48,1024]{3,2,1,0:T(8,128)} %bitcast.104, s32[]{:T(128)S(6)} %select_n.280, s32[]{:T(128)S(6)} %select_n.286, ...), kind=kLoop, calls=%fused_computation.19 | loop fusion | bytes 4718616 | tf_op jit(solution)/shard_map/jit(dynamic_index_in_dim)/squeeze | solution.py:24
  93.4 3.6 %collective-permute-start.29 = (f32[2,48,1024]{2,1,0:T(8,128)}, f32[2,48,1024]{2,1,0:T(8,128)}, u32[]{:S(2)}, u32[]{:S(2)}) collective-permute-start(f32[2,48,1024]{2,1,0:T(8,128)} %get-tuple-element.19), channel_id=1, source_target_pairs={{0,24},{8,0},{16,8},{24,16},{1,25},{9,1},{17,9},{25,17},{2,26},{10... | collective-permute-start | bytes 1179656 | tf_op jit(solution)/shard_map/ppermute | solution.py:41
  98.8 2.4 %bitcast_add_fusion.2 = (f32[2,48,1024]{2,1,0:T(8,128)}, f32[2,48,1024]{2,1,0:T(8,128)}) fusion(f32[2,48,1024]{2,1,0:T(8,128)} %collective-permute-done.27, f32[8,2,48,1024]{3,2,1,0:T(8,128)} %bitcast.105, s32[]{:T(128)S(6)} %select_n.276, f32[2,48,1024]{2,1,0:T(8,128)} %collective-permute-done.30, s32[]{:T(128)S(6)} %select_n.282), kind=kLoop, calls=%fused_computation.16 | loop fusion | flops 196608 | bytes 2359304 | tf_op jit(solution)/shard_map/add | solution.py:42
  105.6 3.0 %collective-permute-start.31 = (f32[2,48,1024]{2,1,0:T(8,128)}, f32[2,48,1024]{2,1,0:T(8,128)}, u32[]{:S(2)}, u32[]{:S(2)}) collective-permute-start(f32[2,48,1024]{2,1,0:T(8,128)} %get-tuple-element.26), channel_id=1, source_target_pairs={{0,24},{8,0},{16,8},{24,16},{1,25},{9,1},{17,9},{25,17},{2,26},{10... | collective-permute-start | bytes 1179656 | tf_op jit(solution)/shard_map/ppermute | solution.py:43
  111.2 3.2 %collective-permute-start.25 = (f32[24,1024]{1,0:T(8,128)S(1)}, f32[24,1024]{1,0:T(8,128)S(1)}, u32[]{:S(2)}, u32[]{:S(2)}) collective-permute-start(f32[24,1024]{1,0:T(8,128)S(1)} %get-tuple-element.30), channel_id=1, source_target_pairs={{0,24},{8,0},{16,8},{24,16},{1,25},{9,1},{17,9},{25,17},{2,26},{10... | collective-permute-start | bytes 294920 | tf_op jit(solution)/shard_map/ppermute | solution.py:34
  114.4 3.7 %collective-permute-done.28 = f32[2,48,1024]{2,1,0:T(8,128)} collective-permute-done((f32[2,48,1024]{2,1,0:T(8,128)}, f32[2,48,1024]{2,1,0:T(8,128)}, u32[]{:S(2)}, u32[]{:S(2)}) %collective-permute-start.28) | collective-permute-done | bytes 393248 | tf_op jit(solution)/shard_map/ppermute | solution.py:42
  122.9 3.2 %collective-permute-start.26 = (f32[48,1024]{1,0:T(8,128)S(1)}, f32[48,1024]{1,0:T(8,128)S(1)}, u32[]{:S(2)}, u32[]{:S(2)}) collective-permute-start(f32[48,1024]{1,0:T(8,128)S(1)} %get-tuple-element.28), channel_id=1, source_target_pairs={{0,24},{8,0},{16,8},{24,16},{1,25},{9,1},{17,9},{25,17},{2,26},{10... | collective-permute-start | bytes 589832 | tf_op jit(solution)/shard_map/ppermute | solution.py:38
  131.6 2.7 %collective-permute-done.34 = f32[48,1024]{1,0:T(8,128)S(1)} collective-permute-done((f32[48,1024]{1,0:T(8,128)S(1)}, f32[48,1024]{1,0:T(8,128)S(1)}, u32[]{:S(2)}, u32[]{:S(2)}) %collective-permute-start.34) | collective-permute-done | bytes 196640 | tf_op jit(solution)/shard_map/ppermute | solution.py:37
  136.9 3.9 %all-to-all-start = ((f32[8,3,4,1024]{3,2,1,0:T(4,128)}), f32[8,3,4,1024]{3,2,1,0:T(4,128)S(1)}, u32[]{:S(2)}, u32[]{:S(2)}) async-start(f32[8,3,4,1024]{3,2,1,0:T(4,128)} %reshape.63), calls=%async_computation | async-start | bytes 786432 | tf_op jit(solution)/shard_map/all_to_all | solution.py:224
  141.0 11.9 %all-to-all-done = f32[8,3,4,1024]{3,2,1,0:T(4,128)S(1)} async-done(((f32[8,3,4,1024]{3,2,1,0:T(4,128)}), f32[8,3,4,1024]{3,2,1,0:T(4,128)S(1)}, u32[]{:S(2)}, u32[]{:S(2)}) %all-to-all-start) | async-done | bytes 393248 | tf_op jit(solution)/shard_map/all_to_all | solution.py:224
  154.7 12.2 %all_to_all.10 = bf16[8,3,4,1024]{3,2,1,0:T(4,128)(2,1)S(1)} all-to-all(bf16[8,3,4,1024]{3,2,1,0:T(4,128)(2,1)S(1)} %copy.37), channel_id=1, replica_groups=mesh['z'=8,'y'=4,'x'=4,'c'=2] {'z'}, dimensions={0} | all-to-all | bytes 393216 | tf_op jit(solution)/shard_map/all_to_all | solution.py:226
  (116 shorter events, 53.0 us)
Async XLA Ops:
  0.0 54.1 %collective-permute-start.15 = (bf16[1024,1024]{1,0:T(8,128)(2,1)}, bf16[1024,1024]{1,0:T(8,128)(2,1)}, u32[]{:S(2)}, u32[]{:S(2)}) collective-permute-start(bf16[1024,1024]{1,0:T(8,128)(2,1)} %param.6), channel_id=1, source_target_pairs={{0,1},{1,0},{2,3},{3,2},{4,5},{5,4},{6,7},{7,6},{8,9},{9,8},{10,11... | collective-permute-start | bytes 6291464 | tf_op jit(solution)/shard_map/ppermute | solution.py:168
  1.2 15.6 %collective-permute-start.2 = (bf16[192,1024]{1,0:T(8,128)(2,1)S(1)}, bf16[192,1024]{1,0:T(8,128)(2,1)S(1)}, u32[]{:S(2)}, u32[]{:S(2)}) collective-permute-start(bf16[192,1024]{1,0:T(8,128)(2,1)S(1)} %bitcast.109), channel_id=1, source_target_pairs={{0,225},{1,224},{32,1},{33,0},{64,33},{65,32},{96,65},{97,64},{128... | collective-permute-start | bytes 1179656 | tf_op jit(solution)/shard_map/ppermute | solution.py:192
  7.2 13.2 %collective-permute-start.6 = (bf16[192,1024]{1,0:T(8,128)(2,1)S(1)}, bf16[192,1024]{1,0:T(8,128)(2,1)S(1)}, u32[]{:S(2)}, u32[]{:S(2)}) collective-permute-start(bf16[192,1024]{1,0:T(8,128)(2,1)S(1)} %bitcast.100), channel_id=1, source_target_pairs={{0,32},{32,64},{64,96},{96,128},{128,160},{160,192},{192,224},{224... | collective-permute-start | bytes 1179656 | tf_op jit(solution)/shard_map/ppermute | solution.py:194
  7.2 19.7 %collective-permute-start.11 = (bf16[192,1024]{1,0:T(8,128)(2,1)S(1)}, bf16[192,1024]{1,0:T(8,128)(2,1)S(1)}, u32[]{:S(2)}, u32[]{:S(2)}) collective-permute-start(bf16[192,1024]{1,0:T(8,128)(2,1)S(1)} %bitcast.110), channel_id=1, source_target_pairs={{0,33},{1,32},{32,65},{33,64},{64,97},{65,96},{96,129},{97,128},{1... | collective-permute-start | bytes 1179656 | tf_op jit(solution)/shard_map/ppermute | solution.py:192
  8.5 18.4 %collective-permute-start = (bf16[192,1024]{1,0:T(8,128)(2,1)S(1)}, bf16[192,1024]{1,0:T(8,128)(2,1)S(1)}, u32[]{:S(2)}, u32[]{:S(2)}) collective-permute-start(bf16[192,1024]{1,0:T(8,128)(2,1)S(1)} %bitcast.101), channel_id=1, source_target_pairs={{0,224},{32,0},{64,32},{96,64},{128,96},{160,128},{192,160},{224,1... | collective-permute-start | bytes 1179656 | tf_op jit(solution)/shard_map/ppermute | solution.py:194
  16.7 16.9 %collective-permute-start.3 = (bf16[192,1024]{1,0:T(8,128)(2,1)S(1)}, bf16[192,1024]{1,0:T(8,128)(2,1)S(1)}, u32[]{:S(2)}, u32[]{:S(2)}) collective-permute-start(bf16[192,1024]{1,0:T(8,128)(2,1)S(1)} %collective-permute-done.2.refs_7_), channel_id=1, source_target_pairs={{0,224},{32,0},{64,32},{96,64},{128,96},{160,128},{192,160},{224,1... | collective-permute-start | bytes 1179656 | tf_op jit(solution)/shard_map/ppermute | solution.py:194
  20.4 16.9 %collective-permute-start.7 = (bf16[192,1024]{1,0:T(8,128)(2,1)S(1)}, bf16[192,1024]{1,0:T(8,128)(2,1)S(1)}, u32[]{:S(2)}, u32[]{:S(2)}) collective-permute-start(bf16[192,1024]{1,0:T(8,128)(2,1)S(1)} %collective-permute-done.6.refs_2_), channel_id=1, source_target_pairs={{0,32},{32,64},{64,96},{96,128},{128,160},{160,192},{192,224},{224... | collective-permute-start | bytes 1179656 | tf_op jit(solution)/shard_map/ppermute | solution.py:194
  26.9 18.8 %collective-permute-start.12 = (bf16[192,1024]{1,0:T(8,128)(2,1)S(1)}, bf16[192,1024]{1,0:T(8,128)(2,1)S(1)}, u32[]{:S(2)}, u32[]{:S(2)}) collective-permute-start(bf16[192,1024]{1,0:T(8,128)(2,1)S(1)} %collective-permute-done.11.refs_3_), channel_id=1, source_target_pairs={{0,32},{32,64},{64,96},{96,128},{128,160},{160,192},{192,224},{224... | collective-permute-start | bytes 1179656 | tf_op jit(solution)/shard_map/ppermute | solution.py:194
  26.9 18.8 %collective-permute-start.1 = (bf16[192,1024]{1,0:T(8,128)(2,1)S(1)}, bf16[192,1024]{1,0:T(8,128)(2,1)S(1)}, u32[]{:S(2)}, u32[]{:S(2)}) collective-permute-start(bf16[192,1024]{1,0:T(8,128)(2,1)S(1)} %collective-permute-done.refs_6_), channel_id=1, source_target_pairs={{0,224},{32,0},{64,32},{96,64},{128,96},{160,128},{192,160},{224,1... | collective-permute-start | bytes 1179656 | tf_op jit(solution)/shard_map/ppermute | solution.py:194
  33.6 16.2 %collective-permute-start.5 = (bf16[192,1024]{1,0:T(8,128)(2,1)S(1)}, bf16[192,1024]{1,0:T(8,128)(2,1)S(1)}, u32[]{:S(2)}, u32[]{:S(2)}) collective-permute-start(bf16[192,1024]{1,0:T(8,128)(2,1)S(1)} %collective-permute-done.3.refs_1_), channel_id=1, source_target_pairs={{0,224},{32,0},{64,32},{96,64},{128,96},{160,128},{192,160},{224,1... | collective-permute-start | bytes 1179656 | tf_op jit(solution)/shard_map/ppermute | solution.py:194
  37.3 16.8 %collective-permute-start.8 = (bf16[192,1024]{1,0:T(8,128)(2,1)S(1)}, bf16[192,1024]{1,0:T(8,128)(2,1)S(1)}, u32[]{:S(2)}, u32[]{:S(2)}) collective-permute-start(bf16[192,1024]{1,0:T(8,128)(2,1)S(1)} %collective-permute-done.7.refs_0_), channel_id=1, source_target_pairs={{0,32},{32,64},{64,96},{96,128},{128,160},{160,192},{192,224},{224... | collective-permute-start | bytes 1179656 | tf_op jit(solution)/shard_map/ppermute | solution.py:194
  45.7 13.4 %collective-permute-start.16 = (bf16[2,96,1024]{2,1,0:T(8,128)(2,1)S(1)}, bf16[2,96,1024]{2,1,0:T(8,128)(2,1)S(1)}, u32[]{:S(2)}, u32[]{:S(2)}) collective-permute-start(bf16[2,96,1024]{2,1,0:T(8,128)(2,1)S(1)} %bitcast.111), channel_id=1, source_target_pairs={{0,1},{1,0},{2,3},{3,2},{4,5},{5,4},{6,7},{7,6},{8,9},{9,8},{10,11... | collective-permute-start | bytes 1179656 | tf_op jit(solution)/shard_map/ppermute | solution.py:174
  45.7 24.6 %collective-permute-start.13 = (bf16[192,1024]{1,0:T(8,128)(2,1)S(1)}, bf16[192,1024]{1,0:T(8,128)(2,1)S(1)}, u32[]{:S(2)}, u32[]{:S(2)}) collective-permute-start(bf16[192,1024]{1,0:T(8,128)(2,1)S(1)} %collective-permute-done.12.refs_1_), channel_id=1, source_target_pairs={{0,32},{32,64},{64,96},{96,128},{128,160},{160,192},{192,224},{224... | collective-permute-start | bytes 1179656 | tf_op jit(solution)/shard_map/ppermute | solution.py:194
  49.8 20.5 %collective-permute-start.4 = (bf16[192,1024]{1,0:T(8,128)(2,1)S(1)}, bf16[192,1024]{1,0:T(8,128)(2,1)S(1)}, u32[]{:S(2)}, u32[]{:S(2)}) collective-permute-start(bf16[192,1024]{1,0:T(8,128)(2,1)S(1)} %collective-permute-done.1.refs_0_), channel_id=1, source_target_pairs={{0,224},{32,0},{64,32},{96,64},{128,96},{160,128},{192,160},{224,1... | collective-permute-start | bytes 1179656 | tf_op jit(solution)/shard_map/ppermute | solution.py:194
  54.1 16.2 %collective-permute-start.10 = (bf16[192,1024]{1,0:T(8,128)(2,1)S(1)}, bf16[192,1024]{1,0:T(8,128)(2,1)S(1)}, u32[]{:S(2)}, u32[]{:S(2)}) collective-permute-start(bf16[192,1024]{1,0:T(8,128)(2,1)S(1)} %collective-permute-done.5.refs_3_), channel_id=1, source_target_pairs={{0,224},{32,0},{64,32},{96,64},{128,96},{160,128},{192,160},{224,1... | collective-permute-start | bytes 1179656 | tf_op jit(solution)/shard_map/ppermute | solution.py:194
  54.1 16.2 %collective-permute-start.9 = (bf16[192,1024]{1,0:T(8,128)(2,1)S(1)}, bf16[192,1024]{1,0:T(8,128)(2,1)S(1)}, u32[]{:S(2)}, u32[]{:S(2)}) collective-permute-start(bf16[192,1024]{1,0:T(8,128)(2,1)S(1)} %collective-permute-done.8.refs_6_), channel_id=1, source_target_pairs={{0,32},{32,64},{64,96},{96,128},{128,160},{160,192},{192,224},{224... | collective-permute-start | bytes 1179656 | tf_op jit(solution)/shard_map/ppermute | solution.py:194
  84.1 12.9 %collective-permute-start.30 = (f32[2,48,1024]{2,1,0:T(8,128)}, f32[2,48,1024]{2,1,0:T(8,128)}, u32[]{:S(2)}, u32[]{:S(2)}) collective-permute-start(f32[2,48,1024]{2,1,0:T(8,128)} %get-tuple-element.21), channel_id=1, source_target_pairs={{0,24},{8,0},{16,8},{24,16},{1,25},{9,1},{17,9},{25,17},{2,26},{10... | collective-permute-start | bytes 1179656 | tf_op jit(solution)/shard_map/ppermute | solution.py:34
  85.8 15.4 %collective-permute-start.19 = (f32[2,48,1024]{2,1,0:T(8,128)}, f32[2,48,1024]{2,1,0:T(8,128)}, u32[]{:S(2)}, u32[]{:S(2)}) collective-permute-start(f32[2,48,1024]{2,1,0:T(8,128)} %get-tuple-element.13), channel_id=1, source_target_pairs={{0,6},{2,0},{4,2},{6,4},{1,7},{3,1},{5,3},{7,5},{8,14},{10,8},{12,... | collective-permute-start | bytes 1179656 | tf_op jit(solution)/shard_map/ppermute | solution.py:41
  87.8 13.8 %collective-permute-start.22 = (f32[2,48,1024]{2,1,0:T(8,128)}, f32[2,48,1024]{2,1,0:T(8,128)}, u32[]{:S(2)}, u32[]{:S(2)}) collective-permute-start(f32[2,48,1024]{2,1,0:T(8,128)} %get-tuple-element.16), channel_id=1, source_target_pairs={{0,2},{2,4},{4,6},{6,0},{1,3},{3,5},{5,7},{7,1},{8,10},{10,12},{12... | collective-permute-start | bytes 1179656 | tf_op jit(solution)/shard_map/ppermute | solution.py:40
  93.4 17.8 %collective-permute-start.29 = (f32[2,48,1024]{2,1,0:T(8,128)}, f32[2,48,1024]{2,1,0:T(8,128)}, u32[]{:S(2)}, u32[]{:S(2)}) collective-permute-start(f32[2,48,1024]{2,1,0:T(8,128)} %get-tuple-element.19), channel_id=1, source_target_pairs={{0,24},{8,0},{16,8},{24,16},{1,25},{9,1},{17,9},{25,17},{2,26},{10... | collective-permute-start | bytes 1179656 | tf_op jit(solution)/shard_map/ppermute | solution.py:41
  101.2 18.1 %collective-permute-start.32 = (f32[2,48,1024]{2,1,0:T(8,128)}, f32[2,48,1024]{2,1,0:T(8,128)}, u32[]{:S(2)}, u32[]{:S(2)}) collective-permute-start(f32[2,48,1024]{2,1,0:T(8,128)} %get-tuple-element.20), channel_id=1, source_target_pairs={{0,8},{8,16},{16,24},{24,0},{1,9},{9,17},{17,25},{25,1},{2,10},{10... | collective-permute-start | bytes 1179656 | tf_op jit(solution)/shard_map/ppermute | solution.py:40
  101.6 16.5 %collective-permute-start.28 = (f32[2,48,1024]{2,1,0:T(8,128)}, f32[2,48,1024]{2,1,0:T(8,128)}, u32[]{:S(2)}, u32[]{:S(2)}) collective-permute-start(f32[2,48,1024]{2,1,0:T(8,128)} %get-tuple-element.25), channel_id=1, source_target_pairs={{0,8},{8,16},{16,24},{24,0},{1,9},{9,17},{17,25},{25,1},{2,10},{10... | collective-permute-start | bytes 1179656 | tf_op jit(solution)/shard_map/ppermute | solution.py:42
  105.6 13.8 %collective-permute-start.31 = (f32[2,48,1024]{2,1,0:T(8,128)}, f32[2,48,1024]{2,1,0:T(8,128)}, u32[]{:S(2)}, u32[]{:S(2)}) collective-permute-start(f32[2,48,1024]{2,1,0:T(8,128)} %get-tuple-element.26), channel_id=1, source_target_pairs={{0,24},{8,0},{16,8},{24,16},{1,25},{9,1},{17,9},{25,17},{2,26},{10... | collective-permute-start | bytes 1179656 | tf_op jit(solution)/shard_map/ppermute | solution.py:43
  136.9 16.0 %all-to-all-start = ((f32[8,3,4,1024]{3,2,1,0:T(4,128)}), f32[8,3,4,1024]{3,2,1,0:T(4,128)S(1)}, u32[]{:S(2)}, u32[]{:S(2)}) async-start(f32[8,3,4,1024]{3,2,1,0:T(4,128)} %reshape.63), calls=%async_computation | async-start | bytes 786432 | tf_op jit(solution)/shard_map/all_to_all | solution.py:224
  (29 other events, 370.2 us)

commit v3 on v2

--- a/solution.py
+++ b/solution.py
@@ -49,64 +49,62 @@
 
 
 def product_kernel(size, count, *refs):
-    blocks, given = refs[: 2 * count], refs[2 * count : 2 * count + 2]
-    *out_refs, a_ref, v_own, v_other, sems = refs[-6:]
-    v_refs = (v_own, v_other)
+    blocks, v_refs = refs[: 2 * count], refs[2 * count : 2 * count + 2]
+    *out_refs, a_ref, sems = refs[-4:]
     rows, k = blocks[0].shape
     half = 2 * size * count
-    copies = [pltpu.make_async_copy(src, dst, sems.at[i]) for i, (src, dst) in enumerate(zip(given, v_refs))]
-    for i, block in enumerate(blocks):
-        level, h = divmod(i, 2)
-        for part in range(2):
-            for pair in range(2):
-                into, of = part * half + (2 * level + pair) * size, pair * rows // 2 + part * size
-                copies.append(
-                    pltpu.make_async_copy(
-                        block.at[of : of + size, :],
-                        a_ref.at[into : into + size, h * k : (h + 1) * k],
-                        sems.at[len(copies)],
+
+    @pl.when(pl.program_id(0) == 0)
+    def _():
+        copies = []
+        for i, block in enumerate(blocks):
+            level, h = divmod(i, 2)
+            for part in range(2):
+                for pair in range(2):
+                    into, of = part * half + (2 * level + pair) * size, pair * rows // 2 + part * size
+                    copies.append(
+                        pltpu.make_async_copy(
+                            block.at[of : of + size, :],
+                            a_ref.at[into : into + size, h * k : (h + 1) * k],
+                            sems.at[len(copies)],
+                        )
                     )
-                )
-    for copy in copies:
-        copy.start()
-    for copy in copies:
-        copy.wait()
-    wide = 512
-
-    def column(n, carry):
-        at = pl.ds(pl.multiple_of(n * wide, wide), wide)
-        sums = sum(
-            lax.dot_general(
-                a_ref[:, h * k : (h + 1) * k], v_ref[at, :], (((1,), (1,)), ((), ())),
-                preferred_element_type=jnp.float32,
-            )
-            for h, v_ref in enumerate(v_refs)
+        for copy in copies:
+            copy.start()
+        for copy in copies:
+            copy.wait()
+
+    sums = sum(
+        lax.dot_general(
+            a_ref[:, h * k : (h + 1) * k], v_ref[...], (((1,), (1,)), ((), ())),
+            preferred_element_type=jnp.float32,
         )
-        for part, out_ref in enumerate(out_refs):
-            out_ref[:, :, at] = sums[part * half : (part + 1) * half].reshape(count, 2 * size, wide)
-        return carry
-
-    lax.fori_loop(0, v_refs[0].shape[0] // wide, column, 0)
+        for h, v_ref in enumerate(v_refs)
+    )
+    for part, out_ref in enumerate(out_refs):
+        out_ref[...] = sums[part * half : (part + 1) * half].reshape(out_ref.shape)
 
 
 def product(blocks, v, group, levels, sums):
     rows, k = blocks[0].shape
     count, size, ab = len(blocks) // 2, rows // 4, v[0].shape[0]
-    place = pl.BlockSpec((count, 2 * size, ab), lambda i: (group, 0, 0))
+    wide = ab // 2
+    place = pl.BlockSpec((count, 2 * size, wide), lambda i: (group, 0, i))
+    columns = pl.BlockSpec((wide, k), lambda i: (i, 0))
+    stay = pl.BlockSpec(memory_space=pl.ANY)
     n = len(blocks) + 2
     return pl.pallas_call(
         functools.partial(product_kernel, size, count),
-        grid=(1,),
+        grid=(2,),
         out_shape=[
             jax.ShapeDtypeStruct((levels, 2 * size, ab), jnp.float32),
             pltpu.HBM((levels, 2 * size, ab), jnp.float32),
         ],
-        in_specs=[pl.BlockSpec(memory_space=pl.ANY)] * (n + len(sums)),
+        in_specs=[stay] * len(blocks) + [columns] * 2 + [stay] * len(sums),
         out_specs=[place] * 2,
         scratch_shapes=[
             pltpu.VMEM((count * rows, 2 * k), v[0].dtype),
-            *[pltpu.VMEM(t.shape, t.dtype) for t in v],
-            pltpu.SemaphoreType.DMA((2 + 4 * len(blocks),)),
+            pltpu.SemaphoreType.DMA((4 * len(blocks),)),
         ],
         input_output_aliases={n + i: i for i in range(len(sums))},
         compiler_params=pltpu.CompilerParams(vmem_limit_bytes=28 << 20),

time: 168 us -> 168 us (level)
  transfers between devices with their start and end apart: 38 -> 38, of which waited for: 18 -> 19; matrix products, arithmetic and copies ran while one was open for 11% -> 11% of each run, Pallas kernels for 4% -> 3%
where the time goes in v3:
time: 168 us; the launch traced here: 167 us
  waiting for transfers between devices  58.6 us (35%)
  starting transfers between devices  56.5 us (34%)
  local copies, waits for them, and re-layouts  13.6 us (8%)
  other arithmetic  13.4 us (8%)
  Pallas kernels  12.4 us (7%)
  blocking collectives  12.2 us (7%)
    ppermute x12, starting transfers between devices, shards(): got = lax.ppermute(moving[h, d], 'z', shift(levels, d))  18.2 us
    ppermute x12, waiting for transfers between devices, shards(): got = lax.ppermute(moving[h, d], 'z', shift(levels, d))  17.3 us
    all_to_all x1, blocking collectives, shards(): return lax.all_to_all(result.reshape(grouped), 'z', 0, 0).reshape(rows, ab)  12.2 us
    all_to_all x1, waiting for transfers between devices, shards(): spread = lax.all_to_all(sums.reshape(grouped), 'z', 0, 0)  11.8 us
    ppermute x2, waiting for transfers between devices, shards(): got = lax.ppermute(moving[h, d], ('z', 'c'), cross(levels, d))  11.5 us
    pallas_call x2, Pallas kernels, product(): pl.pallas_call(functools.partial(product_kernel, size, count), grid=(2,),...  11.3 us
    ppermute x4, starting transfers between devices, scatter_ring(): from_down = send_down(far[half:])  6.71 us
    ppermute x2, waiting for transfers between devices, scatter_ring(): up = send_up(up[:half] + from_up)  6.49 us
  transfers between devices with their start and end apart: 38, of which 19 were waited for; matrix products, arithmetic and copies ran while one was open for 11% of the time, Pallas kernels for 3%

profile of v3, /device:TPU:6, one launch (start us, length us, event | category | flops | bytes accessed | tf_op | source)
XLA Modules:
  0.0 167.1 jit_solution(2093274251218282229)
XLA Ops:
  1.2 6.0 %collective-permute-start.2 = (bf16[192,1024]{1,0:T(8,128)(2,1)S(1)}, bf16[192,1024]{1,0:T(8,128)(2,1)S(1)}, u32[]{:S(2)}, u32[]{:S(2)}) collective-permute-start(bf16[192,1024]{1,0:T(8,128)(2,1)S(1)} %bitcast.109), channel_id=1, source_target_pairs={{0,225},{1,224},{32,1},{33,0},{64,33},{65,32},{96,65},{97,64},{128... | collective-permute-start | bytes 1179656 | tf_op jit(solution)/shard_map/ppermute | solution.py:190
  8.5 3.2 %collective-permute-start = (bf16[192,1024]{1,0:T(8,128)(2,1)S(1)}, bf16[192,1024]{1,0:T(8,128)(2,1)S(1)}, u32[]{:S(2)}, u32[]{:S(2)}) collective-permute-start(bf16[192,1024]{1,0:T(8,128)(2,1)S(1)} %bitcast.101), channel_id=1, source_target_pairs={{0,224},{32,0},{64,32},{96,64},{128,96},{160,128},{192,160},{224,1... | collective-permute-start | bytes 1179656 | tf_op jit(solution)/shard_map/ppermute | solution.py:192
  11.8 5.0 %collective-permute-done.2.refs_7_ = bf16[192,1024]{1,0:T(8,128)(2,1)S(1)} collective-permute-done((bf16[192,1024]{1,0:T(8,128)(2,1)S(1)}, bf16[192,1024]{1,0:T(8,128)(2,1)S(1)}, u32[]{:S(2)}, u32[]{:S(2)}) %collective-permute-start.2) | collective-permute-done | bytes 393248 | tf_op jit(solution)/shard_map/ppermute | solution.py:190
  20.4 6.5 %collective-permute-done.11.refs_3_ = bf16[192,1024]{1,0:T(8,128)(2,1)S(1)} collective-permute-done((bf16[192,1024]{1,0:T(8,128)(2,1)S(1)}, bf16[192,1024]{1,0:T(8,128)(2,1)S(1)}, u32[]{:S(2)}, u32[]{:S(2)}) %collective-permute-start.11) | collective-permute-done | bytes 393248 | tf_op jit(solution)/shard_map/ppermute | solution.py:190
  26.9 3.2 %collective-permute-start.1 = (bf16[192,1024]{1,0:T(8,128)(2,1)S(1)}, bf16[192,1024]{1,0:T(8,128)(2,1)S(1)}, u32[]{:S(2)}, u32[]{:S(2)}) collective-permute-start(bf16[192,1024]{1,0:T(8,128)(2,1)S(1)} %collective-permute-done.refs_6_), channel_id=1, source_target_pairs={{0,224},{32,0},{64,32},{96,64},{128,96},{160,128},{192,160},{224,1... | collective-permute-start | bytes 1179656 | tf_op jit(solution)/shard_map/ppermute | solution.py:192
  30.2 3.4 %collective-permute-done.3.refs_1_ = bf16[192,1024]{1,0:T(8,128)(2,1)S(1)} collective-permute-done((bf16[192,1024]{1,0:T(8,128)(2,1)S(1)}, bf16[192,1024]{1,0:T(8,128)(2,1)S(1)}, u32[]{:S(2)}, u32[]{:S(2)}) %collective-permute-start.3) | collective-permute-done | bytes 393248 | tf_op jit(solution)/shard_map/ppermute | solution.py:192
  33.6 3.7 %collective-permute-start.5 = (bf16[192,1024]{1,0:T(8,128)(2,1)S(1)}, bf16[192,1024]{1,0:T(8,128)(2,1)S(1)}, u32[]{:S(2)}, u32[]{:S(2)}) collective-permute-start(bf16[192,1024]{1,0:T(8,128)(2,1)S(1)} %collective-permute-done.3.refs_1_), channel_id=1, source_target_pairs={{0,224},{32,0},{64,32},{96,64},{128,96},{160,128},{192,160},{224,1... | collective-permute-start | bytes 1179656 | tf_op jit(solution)/shard_map/ppermute | solution.py:192
  38.2 7.5 %collective-permute-done.12.refs_1_ = bf16[192,1024]{1,0:T(8,128)(2,1)S(1)} collective-permute-done((bf16[192,1024]{1,0:T(8,128)(2,1)S(1)}, bf16[192,1024]{1,0:T(8,128)(2,1)S(1)}, u32[]{:S(2)}, u32[]{:S(2)}) %collective-permute-start.12) | collective-permute-done | bytes 393248 | tf_op jit(solution)/shard_map/ppermute | solution.py:192
  45.7 4.0 %collective-permute-done.5.refs_3_ = bf16[192,1024]{1,0:T(8,128)(2,1)S(1)} collective-permute-done((bf16[192,1024]{1,0:T(8,128)(2,1)S(1)}, bf16[192,1024]{1,0:T(8,128)(2,1)S(1)}, u32[]{:S(2)}, u32[]{:S(2)}) %collective-permute-start.5) | collective-permute-done | bytes 393248 | tf_op jit(solution)/shard_map/ppermute | solution.py:192
  49.8 3.7 %collective-permute-start.4 = (bf16[192,1024]{1,0:T(8,128)(2,1)S(1)}, bf16[192,1024]{1,0:T(8,128)(2,1)S(1)}, u32[]{:S(2)}, u32[]{:S(2)}) collective-permute-start(bf16[192,1024]{1,0:T(8,128)(2,1)S(1)} %collective-permute-done.1.refs_0_), channel_id=1, source_target_pairs={{0,224},{32,0},{64,32},{96,64},{128,96},{160,128},{192,160},{224,1... | collective-permute-start | bytes 1179656 | tf_op jit(solution)/shard_map/ppermute | solution.py:192
  56.2 2.9 %compare_select_fusion = (bf16[1024,1024]{1,0:T(8,128)(2,1)S(1)}, bf16[1024,1024]{1,0:T(8,128)(2,1)S(1)}) fusion(bf16[1024,1024]{1,0:T(8,128)(2,1)} %collective-permute-done.15, s32[1024]{0:T(1024)S(1)} %broadcast_bitcast_fusion, s32[1024]{0:T(1024)S(1)} %get-tuple-element.40, bf16[1024,1024]{1,0:T(8,128)(2,1)} %param.6, s32[1024]{0:T(1024)S(1)} %get-tuple-element.39), kind=kLoop, calls=%fused_computation | loop fusion | flops 4194304 | bytes 8400896 | tf_op jit(solution)/shard_map/jit(_where)/select_n | solution.py:163
  64.1 5.7 %shard_map.55 = (f32[8,96,1024]{2,1,0:T(8,128)S(1)}, f32[8,96,1024]{2,1,0:T(8,128)}) custom-call(bf16[192,1024]{1,0:T(8,128)(2,1)S(1)} %copy-done.11, bf16[192,1024]{1,0:T(8,128)(2,1)S(1)} %collective-permute-done.12.refs_1_, bf16[192,1024]{1,0:T(8,128)(2,1)S(1)} %copy-done.5, bf16[192,1024]{1,0:T(8,128)(2,1)S(1)} %copy-done.7, ...), custom_call_target="tpu_custom_call" | custom-call | flops 3221225472 | bytes 10485760 | tf_op jit(solution)/shard_map/pallas_call | solution.py:96
  70.0 5.7 %shard_map.56 = (f32[8,96,1024]{2,1,0:T(8,128)S(1)}, f32[8,96,1024]{2,1,0:T(8,128)}) custom-call(bf16[192,1024]{1,0:T(8,128)(2,1)S(1)} %collective-permute-done.1.refs_0_, bf16[192,1024]{1,0:T(8,128)(2,1)S(1)} %copy-done.1, bf16[192,1024]{1,0:T(8,128)(2,1)S(1)} %collective-permute-done.4.refs_2_, ...), custom_call_target="tpu_custom_call", output_to_operand_aliasing={{0}: (10, {}), {1}: (11, {})} | custom-call | flops 3221225472 | bytes 10485760 | tf_op jit(solution)/shard_map/pallas_call | solution.py:96
  78.9 2.9 %dynamic-slice_bitcast_fusion.8 = (f32[2,48,1024]{2,1,0:T(8,128)}, f32[2,48,1024]{2,1,0:T(8,128)}, f32[2,48,1024]{2,1,0:T(8,128)}, f32[2,48,1024]{2,1,0:T(8,128)...) fusion(f32[8,2,48,1024]{3,2,1,0:T(8,128)} %bitcast.104, s32[]{:T(128)S(6)} %select_n.280, s32[]{:T(128)S(6)} %select_n.286, ...), kind=kLoop, calls=%fused_computation.19 | loop fusion | bytes 4718616 | tf_op jit(solution)/shard_map/jit(dynamic_index_in_dim)/squeeze | solution.py:24
  93.0 3.3 %collective-permute-start.29 = (f32[2,48,1024]{2,1,0:T(8,128)}, f32[2,48,1024]{2,1,0:T(8,128)}, u32[]{:S(2)}, u32[]{:S(2)}) collective-permute-start(f32[2,48,1024]{2,1,0:T(8,128)} %get-tuple-element.19), channel_id=1, source_target_pairs={{0,24},{8,0},{16,8},{24,16},{1,25},{9,1},{17,9},{25,17},{2,26},{10... | collective-permute-start | bytes 1179656 | tf_op jit(solution)/shard_map/ppermute | solution.py:41
  102.5 3.0 %collective-permute-done.18 = f32[2,48,1024]{2,1,0:T(8,128)} collective-permute-done((f32[2,48,1024]{2,1,0:T(8,128)}, f32[2,48,1024]{2,1,0:T(8,128)}, u32[]{:S(2)}, u32[]{:S(2)}) %collective-permute-start.18) | collective-permute-done | bytes 393248 | tf_op jit(solution)/shard_map/ppermute | solution.py:42
  105.4 3.0 %collective-permute-start.31 = (f32[2,48,1024]{2,1,0:T(8,128)}, f32[2,48,1024]{2,1,0:T(8,128)}, u32[]{:S(2)}, u32[]{:S(2)}) collective-permute-start(f32[2,48,1024]{2,1,0:T(8,128)} %get-tuple-element.26), channel_id=1, source_target_pairs={{0,24},{8,0},{16,8},{24,16},{1,25},{9,1},{17,9},{25,17},{2,26},{10... | collective-permute-start | bytes 1179656 | tf_op jit(solution)/shard_map/ppermute | solution.py:43
  111.1 3.2 %collective-permute-start.25 = (f32[24,1024]{1,0:T(8,128)S(1)}, f32[24,1024]{1,0:T(8,128)S(1)}, u32[]{:S(2)}, u32[]{:S(2)}) collective-permute-start(f32[24,1024]{1,0:T(8,128)S(1)} %get-tuple-element.30), channel_id=1, source_target_pairs={{0,24},{8,0},{16,8},{24,16},{1,25},{9,1},{17,9},{25,17},{2,26},{10... | collective-permute-start | bytes 294920 | tf_op jit(solution)/shard_map/ppermute | solution.py:34
  114.3 3.5 %collective-permute-done.28 = f32[2,48,1024]{2,1,0:T(8,128)} collective-permute-done((f32[2,48,1024]{2,1,0:T(8,128)}, f32[2,48,1024]{2,1,0:T(8,128)}, u32[]{:S(2)}, u32[]{:S(2)}) %collective-permute-start.28) | collective-permute-done | bytes 393248 | tf_op jit(solution)/shard_map/ppermute | solution.py:42
  122.6 3.2 %collective-permute-start.26 = (f32[48,1024]{1,0:T(8,128)S(1)}, f32[48,1024]{1,0:T(8,128)S(1)}, u32[]{:S(2)}, u32[]{:S(2)}) collective-permute-start(f32[48,1024]{1,0:T(8,128)S(1)} %get-tuple-element.28), channel_id=1, source_target_pairs={{0,24},{8,0},{16,8},{24,16},{1,25},{9,1},{17,9},{25,17},{2,26},{10... | collective-permute-start | bytes 589832 | tf_op jit(solution)/shard_map/ppermute | solution.py:38
  131.8 2.7 %collective-permute-done.34 = f32[48,1024]{1,0:T(8,128)S(1)} collective-permute-done((f32[48,1024]{1,0:T(8,128)S(1)}, f32[48,1024]{1,0:T(8,128)S(1)}, u32[]{:S(2)}, u32[]{:S(2)}) %collective-permute-start.34) | collective-permute-done | bytes 196640 | tf_op jit(solution)/shard_map/ppermute | solution.py:37
  136.9 3.5 %all-to-all-start = ((f32[8,3,4,1024]{3,2,1,0:T(4,128)}), f32[8,3,4,1024]{3,2,1,0:T(4,128)S(1)}, u32[]{:S(2)}, u32[]{:S(2)}) async-start(f32[8,3,4,1024]{3,2,1,0:T(4,128)} %reshape.63), calls=%async_computation | async-start | bytes 786432 | tf_op jit(solution)/shard_map/all_to_all | solution.py:222
  140.6 11.8 %all-to-all-done = f32[8,3,4,1024]{3,2,1,0:T(4,128)S(1)} async-done(((f32[8,3,4,1024]{3,2,1,0:T(4,128)}), f32[8,3,4,1024]{3,2,1,0:T(4,128)S(1)}, u32[]{:S(2)}, u32[]{:S(2)}) %all-to-all-start) | async-done | bytes 393248 | tf_op jit(solution)/shard_map/all_to_all | solution.py:222
  154.2 12.2 %all_to_all.10 = bf16[8,3,4,1024]{3,2,1,0:T(4,128)(2,1)S(1)} all-to-all(bf16[8,3,4,1024]{3,2,1,0:T(4,128)(2,1)S(1)} %copy.37), channel_id=1, replica_groups=mesh['z'=8,'y'=4,'x'=4,'c'=2] {'z'}, dimensions={0} | all-to-all | bytes 393216 | tf_op jit(solution)/shard_map/all_to_all | solution.py:224
  (116 shorter events, 53.9 us)
Async XLA Ops:
  0.0 54.1 %collective-permute-start.15 = (bf16[1024,1024]{1,0:T(8,128)(2,1)}, bf16[1024,1024]{1,0:T(8,128)(2,1)}, u32[]{:S(2)}, u32[]{:S(2)}) collective-permute-start(bf16[1024,1024]{1,0:T(8,128)(2,1)} %param.6), channel_id=1, source_target_pairs={{0,1},{1,0},{2,3},{3,2},{4,5},{5,4},{6,7},{7,6},{8,9},{9,8},{10,11... | collective-permute-start | bytes 6291464 | tf_op jit(solution)/shard_map/ppermute | solution.py:166
  1.2 15.6 %collective-permute-start.2 = (bf16[192,1024]{1,0:T(8,128)(2,1)S(1)}, bf16[192,1024]{1,0:T(8,128)(2,1)S(1)}, u32[]{:S(2)}, u32[]{:S(2)}) collective-permute-start(bf16[192,1024]{1,0:T(8,128)(2,1)S(1)} %bitcast.109), channel_id=1, source_target_pairs={{0,225},{1,224},{32,1},{33,0},{64,33},{65,32},{96,65},{97,64},{128... | collective-permute-start | bytes 1179656 | tf_op jit(solution)/shard_map/ppermute | solution.py:190
  7.2 13.2 %collective-permute-start.6 = (bf16[192,1024]{1,0:T(8,128)(2,1)S(1)}, bf16[192,1024]{1,0:T(8,128)(2,1)S(1)}, u32[]{:S(2)}, u32[]{:S(2)}) collective-permute-start(bf16[192,1024]{1,0:T(8,128)(2,1)S(1)} %bitcast.100), channel_id=1, source_target_pairs={{0,32},{32,64},{64,96},{96,128},{128,160},{160,192},{192,224},{224... | collective-permute-start | bytes 1179656 | tf_op jit(solution)/shard_map/ppermute | solution.py:192
  7.2 19.7 %collective-permute-start.11 = (bf16[192,1024]{1,0:T(8,128)(2,1)S(1)}, bf16[192,1024]{1,0:T(8,128)(2,1)S(1)}, u32[]{:S(2)}, u32[]{:S(2)}) collective-permute-start(bf16[192,1024]{1,0:T(8,128)(2,1)S(1)} %bitcast.110), channel_id=1, source_target_pairs={{0,33},{1,32},{32,65},{33,64},{64,97},{65,96},{96,129},{97,128},{1... | collective-permute-start | bytes 1179656 | tf_op jit(solution)/shard_map/ppermute | solution.py:190
  8.5 18.4 %collective-permute-start = (bf16[192,1024]{1,0:T(8,128)(2,1)S(1)}, bf16[192,1024]{1,0:T(8,128)(2,1)S(1)}, u32[]{:S(2)}, u32[]{:S(2)}) collective-permute-start(bf16[192,1024]{1,0:T(8,128)(2,1)S(1)} %bitcast.101), channel_id=1, source_target_pairs={{0,224},{32,0},{64,32},{96,64},{128,96},{160,128},{192,160},{224,1... | collective-permute-start | bytes 1179656 | tf_op jit(solution)/shard_map/ppermute | solution.py:192
  16.7 16.9 %collective-permute-start.3 = (bf16[192,1024]{1,0:T(8,128)(2,1)S(1)}, bf16[192,1024]{1,0:T(8,128)(2,1)S(1)}, u32[]{:S(2)}, u32[]{:S(2)}) collective-permute-start(bf16[192,1024]{1,0:T(8,128)(2,1)S(1)} %collective-permute-done.2.refs_7_), channel_id=1, source_target_pairs={{0,224},{32,0},{64,32},{96,64},{128,96},{160,128},{192,160},{224,1... | collective-permute-start | bytes 1179656 | tf_op jit(solution)/shard_map/ppermute | solution.py:192
  20.4 16.9 %collective-permute-start.7 = (bf16[192,1024]{1,0:T(8,128)(2,1)S(1)}, bf16[192,1024]{1,0:T(8,128)(2,1)S(1)}, u32[]{:S(2)}, u32[]{:S(2)}) collective-permute-start(bf16[192,1024]{1,0:T(8,128)(2,1)S(1)} %collective-permute-done.6.refs_2_), channel_id=1, source_target_pairs={{0,32},{32,64},{64,96},{96,128},{128,160},{160,192},{192,224},{224... | collective-permute-start | bytes 1179656 | tf_op jit(solution)/shard_map/ppermute | solution.py:192
  26.9 18.8 %collective-permute-start.12 = (bf16[192,1024]{1,0:T(8,128)(2,1)S(1)}, bf16[192,1024]{1,0:T(8,128)(2,1)S(1)}, u32[]{:S(2)}, u32[]{:S(2)}) collective-permute-start(bf16[192,1024]{1,0:T(8,128)(2,1)S(1)} %collective-permute-done.11.refs_3_), channel_id=1, source_target_pairs={{0,32},{32,64},{64,96},{96,128},{128,160},{160,192},{192,224},{224... | collective-permute-start | bytes 1179656 | tf_op jit(solution)/shard_map/ppermute | solution.py:192
  26.9 18.8 %collective-permute-start.1 = (bf16[192,1024]{1,0:T(8,128)(2,1)S(1)}, bf16[192,1024]{1,0:T(8,128)(2,1)S(1)}, u32[]{:S(2)}, u32[]{:S(2)}) collective-permute-start(bf16[192,1024]{1,0:T(8,128)(2,1)S(1)} %collective-permute-done.refs_6_), channel_id=1, source_target_pairs={{0,224},{32,0},{64,32},{96,64},{128,96},{160,128},{192,160},{224,1... | collective-permute-start | bytes 1179656 | tf_op jit(solution)/shard_map/ppermute | solution.py:192
  33.6 16.2 %collective-permute-start.5 = (bf16[192,1024]{1,0:T(8,128)(2,1)S(1)}, bf16[192,1024]{1,0:T(8,128)(2,1)S(1)}, u32[]{:S(2)}, u32[]{:S(2)}) collective-permute-start(bf16[192,1024]{1,0:T(8,128)(2,1)S(1)} %collective-permute-done.3.refs_1_), channel_id=1, source_target_pairs={{0,224},{32,0},{64,32},{96,64},{128,96},{160,128},{192,160},{224,1... | collective-permute-start | bytes 1179656 | tf_op jit(solution)/shard_map/ppermute | solution.py:192
  37.3 16.8 %collective-permute-start.8 = (bf16[192,1024]{1,0:T(8,128)(2,1)S(1)}, bf16[192,1024]{1,0:T(8,128)(2,1)S(1)}, u32[]{:S(2)}, u32[]{:S(2)}) collective-permute-start(bf16[192,1024]{1,0:T(8,128)(2,1)S(1)} %collective-permute-done.7.refs_0_), channel_id=1, source_target_pairs={{0,32},{32,64},{64,96},{96,128},{128,160},{160,192},{192,224},{224... | collective-permute-start | bytes 1179656 | tf_op jit(solution)/shard_map/ppermute | solution.py:192
  45.7 13.4 %collective-permute-start.16 = (bf16[2,96,1024]{2,1,0:T(8,128)(2,1)S(1)}, bf16[2,96,1024]{2,1,0:T(8,128)(2,1)S(1)}, u32[]{:S(2)}, u32[]{:S(2)}) collective-permute-start(bf16[2,96,1024]{2,1,0:T(8,128)(2,1)S(1)} %bitcast.111), channel_id=1, source_target_pairs={{0,1},{1,0},{2,3},{3,2},{4,5},{5,4},{6,7},{7,6},{8,9},{9,8},{10,11... | collective-permute-start | bytes 1179656 | tf_op jit(solution)/shard_map/ppermute | solution.py:172
  45.7 24.1 %collective-permute-start.13 = (bf16[192,1024]{1,0:T(8,128)(2,1)S(1)}, bf16[192,1024]{1,0:T(8,128)(2,1)S(1)}, u32[]{:S(2)}, u32[]{:S(2)}) collective-permute-start(bf16[192,1024]{1,0:T(8,128)(2,1)S(1)} %collective-permute-done.12.refs_1_), channel_id=1, source_target_pairs={{0,32},{32,64},{64,96},{96,128},{128,160},{160,192},{192,224},{224... | collective-permute-start | bytes 1179656 | tf_op jit(solution)/shard_map/ppermute | solution.py:192
  49.8 20.0 %collective-permute-start.4 = (bf16[192,1024]{1,0:T(8,128)(2,1)S(1)}, bf16[192,1024]{1,0:T(8,128)(2,1)S(1)}, u32[]{:S(2)}, u32[]{:S(2)}) collective-permute-start(bf16[192,1024]{1,0:T(8,128)(2,1)S(1)} %collective-permute-done.1.refs_0_), channel_id=1, source_target_pairs={{0,224},{32,0},{64,32},{96,64},{128,96},{160,128},{192,160},{224,1... | collective-permute-start | bytes 1179656 | tf_op jit(solution)/shard_map/ppermute | solution.py:192
  54.1 15.7 %collective-permute-start.10 = (bf16[192,1024]{1,0:T(8,128)(2,1)S(1)}, bf16[192,1024]{1,0:T(8,128)(2,1)S(1)}, u32[]{:S(2)}, u32[]{:S(2)}) collective-permute-start(bf16[192,1024]{1,0:T(8,128)(2,1)S(1)} %collective-permute-done.5.refs_3_), channel_id=1, source_target_pairs={{0,224},{32,0},{64,32},{96,64},{128,96},{160,128},{192,160},{224,1... | collective-permute-start | bytes 1179656 | tf_op jit(solution)/shard_map/ppermute | solution.py:192
  54.1 15.9 %collective-permute-start.9 = (bf16[192,1024]{1,0:T(8,128)(2,1)S(1)}, bf16[192,1024]{1,0:T(8,128)(2,1)S(1)}, u32[]{:S(2)}, u32[]{:S(2)}) collective-permute-start(bf16[192,1024]{1,0:T(8,128)(2,1)S(1)} %collective-permute-done.8.refs_6_), channel_id=1, source_target_pairs={{0,32},{32,64},{64,96},{96,128},{128,160},{160,192},{192,224},{224... | collective-permute-start | bytes 1179656 | tf_op jit(solution)/shard_map/ppermute | solution.py:192
  85.1 15.4 %collective-permute-start.19 = (f32[2,48,1024]{2,1,0:T(8,128)}, f32[2,48,1024]{2,1,0:T(8,128)}, u32[]{:S(2)}, u32[]{:S(2)}) collective-permute-start(f32[2,48,1024]{2,1,0:T(8,128)} %get-tuple-element.13), channel_id=1, source_target_pairs={{0,6},{2,0},{4,2},{6,4},{1,7},{3,1},{5,3},{7,5},{8,14},{10,8},{12,... | collective-permute-start | bytes 1179656 | tf_op jit(solution)/shard_map/ppermute | solution.py:41
  87.4 13.5 %collective-permute-start.22 = (f32[2,48,1024]{2,1,0:T(8,128)}, f32[2,48,1024]{2,1,0:T(8,128)}, u32[]{:S(2)}, u32[]{:S(2)}) collective-permute-start(f32[2,48,1024]{2,1,0:T(8,128)} %get-tuple-element.16), channel_id=1, source_target_pairs={{0,2},{2,4},{4,6},{6,0},{1,3},{3,5},{5,7},{7,1},{8,10},{10,12},{12... | collective-permute-start | bytes 1179656 | tf_op jit(solution)/shard_map/ppermute | solution.py:40
  93.0 18.1 %collective-permute-start.29 = (f32[2,48,1024]{2,1,0:T(8,128)}, f32[2,48,1024]{2,1,0:T(8,128)}, u32[]{:S(2)}, u32[]{:S(2)}) collective-permute-start(f32[2,48,1024]{2,1,0:T(8,128)} %get-tuple-element.19), channel_id=1, source_target_pairs={{0,24},{8,0},{16,8},{24,16},{1,25},{9,1},{17,9},{25,17},{2,26},{10... | collective-permute-start | bytes 1179656 | tf_op jit(solution)/shard_map/ppermute | solution.py:41
  96.3 13.3 %collective-permute-start.21 = (f32[2,48,1024]{2,1,0:T(8,128)}, f32[2,48,1024]{2,1,0:T(8,128)}, u32[]{:S(2)}, u32[]{:S(2)}) collective-permute-start(f32[2,48,1024]{2,1,0:T(8,128)} %get-tuple-element.18), channel_id=1, source_target_pairs={{0,6},{2,0},{4,2},{6,4},{1,7},{3,1},{5,3},{7,5},{8,14},{10,8},{12,... | collective-permute-start | bytes 1179656 | tf_op jit(solution)/shard_map/ppermute | solution.py:43
  100.5 18.5 %collective-permute-start.32 = (f32[2,48,1024]{2,1,0:T(8,128)}, f32[2,48,1024]{2,1,0:T(8,128)}, u32[]{:S(2)}, u32[]{:S(2)}) collective-permute-start(f32[2,48,1024]{2,1,0:T(8,128)} %get-tuple-element.20), channel_id=1, source_target_pairs={{0,8},{8,16},{16,24},{24,0},{1,9},{9,17},{17,25},{25,1},{2,10},{10... | collective-permute-start | bytes 1179656 | tf_op jit(solution)/shard_map/ppermute | solution.py:40
  100.9 16.9 %collective-permute-start.28 = (f32[2,48,1024]{2,1,0:T(8,128)}, f32[2,48,1024]{2,1,0:T(8,128)}, u32[]{:S(2)}, u32[]{:S(2)}) collective-permute-start(f32[2,48,1024]{2,1,0:T(8,128)} %get-tuple-element.25), channel_id=1, source_target_pairs={{0,8},{8,16},{16,24},{24,0},{1,9},{9,17},{17,25},{25,1},{2,10},{10... | collective-permute-start | bytes 1179656 | tf_op jit(solution)/shard_map/ppermute | solution.py:42
  105.4 13.6 %collective-permute-start.31 = (f32[2,48,1024]{2,1,0:T(8,128)}, f32[2,48,1024]{2,1,0:T(8,128)}, u32[]{:S(2)}, u32[]{:S(2)}) collective-permute-start(f32[2,48,1024]{2,1,0:T(8,128)} %get-tuple-element.26), channel_id=1, source_target_pairs={{0,24},{8,0},{16,8},{24,16},{1,25},{9,1},{17,9},{25,17},{2,26},{10... | collective-permute-start | bytes 1179656 | tf_op jit(solution)/shard_map/ppermute | solution.py:43
  136.9 15.4 %all-to-all-start = ((f32[8,3,4,1024]{3,2,1,0:T(4,128)}), f32[8,3,4,1024]{3,2,1,0:T(4,128)S(1)}, u32[]{:S(2)}, u32[]{:S(2)}) async-start(f32[8,3,4,1024]{3,2,1,0:T(4,128)} %reshape.63), calls=%async_computation | async-start | bytes 786432 | tf_op jit(solution)/shard_map/all_to_all | solution.py:222
  (29 other events, 371.8 us)
